TPU v7x, 32 devices: a whole 2x2x4 slice. The times are simulated.
32 devices in a mesh: blk: 8 (over y, x, core), line: 4 (over z).
Axes of the slice: x: 2, y: 2, z: 4, core: 2. Of those that a mesh axis runs over, the one named last changes fastest.
Arguments:
- state: bfloat16 [32, 88, 256, 128], P('blk', None, 'line'), may hold values from -6 to 6
- speed_in: float32 [32, 256, 128], P('blk', 'line'), may hold values from -1 to 1
- speed_wall: float32 [32, 256, 128], P('blk', 'line'), may hold values from -1 to 1
- density: float32 [32, 256, 128], P('blk', 'line'), may hold values from 0.3 to 3
- rates: bfloat16 [88, 88], replicated, may hold values from -0.625 to 0.625
- wall_op: bfloat16 [256, 256], replicated, may hold values from -0.375 to 0.375
- block_perm: int32 [32], replicated, may hold values from 0 to 31, each once
- patch_src: int32 [32, 2, 16], P('blk', None, 'line'), may hold values from 0 to 63
- patch_flip: int32 [32, 2, 16], P('blk', None, 'line'), may hold values 0 or 1
- patch_wall: int32 [32, 2, 16], P('blk', None, 'line'), may hold values 0 or 1
Outputs:
- next_state: bfloat16 [32, 88, 256, 128], P('blk', None, 'line')
Inputs may be any that keep to these rules, and one draw needn't show every extreme that they name: `block_perm`: each block id 0 to 31 stands in exactly one slot. patch_src // 2 is a block id (not a slot) and patch_src % 2 its face; a patch's rows are the same rows of the source face. `patch_flip`: 1 reverses the order of a patch's rows. `patch_wall`: 1 mirrors the face's own cells in place of a neighbour's.
All inputs are finite; a program needn't handle non-finite values. No bound on the sum of `patch_flip` or of `patch_wall` on one device may be relied on, other than what follows from the above.
Results may differ from a plain program's by a relative error of at most 0.0014.
Values may be sent and summed in bfloat16 or wider, within the bound.
No kernel may reach another device: no remote copies, remote signals or barrier semaphores. Data moves between devices by JAX's collectives and lax.ppermute only.
A program may use at most 192 MiB of HBM per device.

v0:
```python
import math

import jax
import jax.numpy as jnp
from jax import lax
from jax.sharding import PartitionSpec as P

filter_sigma = 0.5
section_step = 0.25
deriv_coef = [5.0 / 6.0, -5.0 / 21.0, 5.0 / 84.0, -5.0 / 504.0, 1.0 / 1260.0]
high_pass = [(-1) ** offset * math.comb(10, 5 + offset) / 1024.0 for offset in range(-5, 6)]


def edge_cells(field):
    columns = field.shape[-1]
    return jnp.stack([field[..., :5], jnp.flip(field[..., columns - 5 :], -1)], 1)


def source_faces(block_perm, patch_src, patch_wall, first_slot):
    nblocks = block_perm.shape[0]
    block_ids = jnp.arange(nblocks, dtype=jnp.int32)
    matches = block_perm[None, :] == block_ids[:, None]
    slot_of = jnp.sum(jnp.where(matches, block_ids[None, :], 0), axis=1)
    owned = patch_src.shape[0]
    own_face = (first_slot + jnp.arange(owned, dtype=jnp.int32))[:, None, None] * 2 + jnp.arange(
        2, dtype=jnp.int32
    )[None, :, None]
    remote = jnp.take(slot_of, patch_src // 2) * 2 + patch_src % 2
    return jnp.where(patch_wall == 1, own_face, remote)


def select_ghosts(gathered, source, flips, patch_count):
    total = gathered.shape[0]
    chans = gathered.shape[2]
    rows = gathered.shape[3]
    flat = gathered.reshape(total * 2, chans, patch_count, rows // patch_count, 5)
    patch_index = jnp.arange(patch_count, dtype=jnp.int32)[None, None, :]
    picked = flat[source, :, patch_index]
    picked = jnp.where(flips[..., None, None, None] == 1, jnp.flip(picked, -2), picked)
    picked = jnp.transpose(picked, (0, 1, 3, 2, 4, 5))
    return picked.reshape(source.shape[0], 2, chans, rows, 5)


def section_update(state, ghosts, normal, speed_in, speed_wall, density, rates):
    values = state.astype(jnp.float32)
    columns = values.shape[-1]
    extended = jnp.concatenate(
        [jnp.flip(ghosts[:, 0].astype(jnp.float32), -1), values, ghosts[:, 1].astype(jnp.float32)],
        -1,
    )
    smooth = values
    for offset in range(11):
        smooth = (
            smooth - filter_sigma * high_pass[offset] * extended[..., offset : offset + columns]
        )
    slope = jnp.zeros_like(values)
    for offset in range(1, 6):
        slope = slope + deriv_coef[offset - 1] * (
            extended[..., 5 + offset : 5 + offset + columns]
            - extended[..., 5 - offset : 5 - offset + columns]
        )
    mixed = jnp.einsum("ce,belp->bclp", rates, state, preferred_element_type=jnp.float32)
    residual = -speed_in[:, None] * slope - speed_wall[:, None] * normal + density[:, None] * mixed
    return (smooth + section_step * residual).astype(jnp.bfloat16)


def body(
    state,
    speed_in,
    speed_wall,
    density,
    rates,
    wall_op,
    block_perm,
    patch_src,
    patch_flip,
    patch_wall,
):
    owned = state.shape[0]
    rows = state.shape[2]
    gathered = lax.all_gather(edge_cells(state), "blk", axis=0, tiled=True)
    source = source_faces(block_perm, patch_src, patch_wall, lax.axis_index("blk") * owned)
    ghosts = select_ghosts(gathered, source, patch_flip, patch_src.shape[2])
    first_row = lax.axis_index("line") * rows
    my_rows = lax.dynamic_slice_in_dim(wall_op, first_row, rows, 0)
    summed = jnp.einsum(
        "lm,bcmp->bclp",
        my_rows,
        lax.all_gather(state, "line", axis=2, tiled=True),
        preferred_element_type=jnp.float32,
    )
    normal = lax.optimization_barrier(summed.astype(jnp.bfloat16))
    return section_update(
        state, ghosts, normal.astype(jnp.float32), speed_in, speed_wall, density, rates
    )


def solution(mesh):
    return jax.shard_map(
        body,
        mesh=mesh,
        in_specs=(
            P("blk", None, "line", None),
            P("blk", "line", None),
            P("blk", "line", None),
            P("blk", "line", None),
            P(),
            P(),
            P(),
            P("blk", None, "line"),
            P("blk", None, "line"),
            P("blk", None, "line"),
        ),
        out_specs=P("blk", None, "line", None),
        check_vma=False,
    )
```

profile of v0, /device:TPU:0, one launch (start us, length us, event | category | flops | bytes accessed | tf_op | source)
XLA Modules:
  0.0 582.6 jit_solution(9919181915388642683)
XLA Ops:
  6.5 0.0 copy-start
  6.5 0.0 all-gather.3.cloned.1.call-start
  6.5 10.9 %fusion.21 = (bf16[4,88,64,5]{3,2,1,0:T(8,128)(2,1)}, bf16[4,88,64,5]{3,2,1,0:T(8,128)(2,1)}) fusion(bf16[4,88,64,128]{3,2,1,0:T(8,128)(2,1)} %param.10), kind=kLoop, calls=%fused_computation.67 | loop fusion | bytes 901120 | tf_op jit(solution)/shard_map/slice | solution.py:16
  17.5 8.2 %copy.32 = bf16[4,88,64,5]{1,2,3,0:T(8,128)(2,1)S(1)} copy(bf16[4,88,64,5]{3,2,1,0:T(8,128)(2,1)} %get-tuple-element.8) | data formatting | bytes 450560
  25.7 8.2 %copy.31 = bf16[4,88,64,5]{1,2,3,0:T(8,128)(2,1)S(1)} copy(bf16[4,88,64,5]{3,2,1,0:T(8,128)(2,1)} %get-tuple-element.7) | data formatting | bytes 450560
  33.9 1.0 pad_maximum_fusion.2
  34.8 0.0 all-gather.3.cloned.1.call-update
  34.9 0.0 copy-start.5
  34.9 0.0 copy-start.8
  34.9 0.2 all-gather.5.cloned.1.call-start
  35.1 0.5 all-gather.5.cloned.1.call-update
  35.6 0.0 copy-start.7
  35.7 0.0 copy-start.3
  35.7 0.0 copy-start.6
  35.7 0.0 copy-start.4
  35.7 8.2 %convert_element_type.27 = f32[4,88,64,128]{3,2,1,0:T(8,128)} convert(bf16[4,88,64,128]{3,2,1,0:T(8,128)(2,1)} %param.10) | non-fusion elementwise | flops 2883584 | bytes 17301504 | tf_op jit(solution)/shard_map/convert_element_type | solution.py:45
  43.9 0.0 copy-done.5
  44.0 0.1 reshape.61
  44.1 0.0 copy-done.8
  44.1 0.1 select_reduce_fusion
  44.2 0.7 gather_fusion
  44.9 0.1 reshape.60
  45.0 0.1 iota_add_fusion
  45.0 0.0 copy-done.7
  45.0 0.1 bitcast_or_fusion
  45.1 0.1 reshape.67
  45.2 0.0 copy-done.3
  45.2 0.0 copy-done.6
  45.3 0.0 copy-done.4
  45.3 11.3 %fusion.13 = f32[4,64,128,88]{2,3,1,0:T(8,128)} fusion(bf16[4,88,64,128]{3,2,1,0:T(8,128)(2,1)} %param.10, bf16[88,88]{1,0:T(8,128)(2,1)S(1)} %copy-done.4), kind=kOutput, calls=%fused_computation.37 | convolution fusion | flops 507510784 | bytes 17316992 | tf_op jit(solution)/shard_map/ce,belp->bclp/dot_general | solution.py:62
  56.6 22.2 %all-gather.3.cloned.1.call-done = bf16[32,2,88,64,5]{2,3,4,1,0:T(8,128)(2,1)} async-done(((bf16[4,2,88,64,5]{2,3,4,1,0:T(8,128)(2,1)}), bf16[32,2,88,64,5]{2,3,4,1,0:T(8,128)(2,1)}) %all-gather.3.cloned.1.call-update) | async-done | bytes 3604496 | tf_op jit(solution)/shard_map/all_gather | solution.py:81
  78.7 3.2 gather_fusion.1
  82.0 0.8 rev.13
  82.8 0.1 select_bitcast_fusion
  82.9 19.2 %copy.26 = bf16[4,2,88,4,16,5]{5,4,3,2,0,1:T(8,128)(2,1)} copy(bf16[4,2,88,4,16,5]{2,4,5,3,1,0:T(8,128)(2,1)S(1)} %select_bitcast_fusion) | data formatting | bytes 901120 | tf_op jit(solution)/shard_map/transpose | solution.py:40
  102.1 12.3 %fusion.12 = (f32[4,88,64,5]{3,2,1,0:T(8,128)}, f32[4,88,64,5]{3,2,1,0:T(8,128)}) fusion(bf16[4,2,88,64,5]{4,3,2,0,1:T(8,128)(2,1)} %bitcast.45), kind=kLoop, calls=%fused_computation.36 | loop fusion | flops 225280 | bytes 1351680 | tf_op jit(solution)/shard_map/convert_element_type | solution.py:48
  114.4 17.6 %rev.14 = f32[4,88,64,5]{3,2,1,0:T(8,128)} reverse(f32[4,88,64,5]{3,2,1,0:T(8,128)} %get-tuple-element.5), dimensions={3} | reverse | bytes 901120 | tf_op jit(solution)/shard_map/jit(_flip)/rev | solution.py:48
  132.1 0.0 copy-start.1
  132.1 0.0 copy-start.2
  132.1 339.3 %all-gather.5.cloned.1.call-done = bf16[4,88,256,128]{3,2,1,0:T(8,128)(2,1)} async-done(((bf16[4,88,64,128]{3,2,1,0:T(8,128)(2,1)}), bf16[4,88,256,128]{3,2,1,0:T(8,128)(2,1)}) %all-gather.5.cloned.1.call-update) | async-done | bytes 23068688 | tf_op jit(solution)/shard_map/all_gather | solution.py:89
  471.4 0.0 copy-done
  471.4 11.7 %convert_bitcast_fusion = bf16[4,88,64,128]{3,2,1,0:T(8,128)(2,1)S(1)} fusion(bf16[4,88,256,128]{3,2,1,0:T(8,128)(2,1)} %all-gather.5.cloned.1.call-done, bf16[256,256]{1,0:T(8,128)(2,1)S(1)} %copy-done, s32[]{:T(128)S(6)} %select_n.47), kind=kOutput, calls=%fused_computation.39 | convolution fusion | flops 1479278592 | bytes 28868612 | tf_op jit(solution)/shard_map/lm,bcmp->bclp/dot_general | solution.py:86
  483.1 0.0 copy-done.1
  483.1 0.0 copy-done.2
  483.1 92.7 %fusion.10 = bf16[4,88,64,128]{3,2,1,0:T(8,128)(2,1)} fusion(f32[4,64,128,88]{2,3,1,0:T(8,128)} %fusion.13, bf16[4,88,64,128]{3,2,1,0:T(8,128)(2,1)S(1)} %convert_bitcast_fusion, f32[4,88,64,5]{3,2,1,0:T(8,128)} %get-tuple-element.6, f32[4,88,64,128]{3,2,1,0:T(8,128)} %convert_element_type.27, f32[4,88,64,5]{3,2,1,0:T(8,128)} %rev.14, ...), kind=kLoop, calls=%fused_computation.31 | loop fusion | flops 158597120 | bytes 35897344 | tf_op jit(solution)/shard_map/convert_element_type | solution.py:64
  (6 shorter events, 0.1 us)
Async XLA Ops:
  6.5 464.9 %copy-start = (bf16[256,256]{1,0:T(8,128)(2,1)S(1)}, bf16[256,256]{1,0:T(8,128)(2,1)}, u32[]{:S(2)}) copy-start(bf16[256,256]{1,0:T(8,128)(2,1)} %param.15) | copy-start | bytes 393220
  6.5 72.2 %all-gather.3.cloned.1.call-start = ((), (), s32[]{:S(2)}) async-start(), calls=%async_computation | async-start | bytes 5898240 | tf_op jit(solution)/shard_map/all_gather | solution.py:81
  34.9 9.1 %copy-start.5 = (s32[4,2,4]{2,1,0:T(2,128)S(1)}, s32[4,2,4]{2,1,0:T(2,128)}, u32[]{:S(2)}) copy-start(s32[4,2,4]{2,1,0:T(2,128)} %param.17) | copy-start | bytes 388
  34.9 9.2 %copy-start.8 = (s32[32]{0:T(128)S(1)}, s32[32]{0:T(128)}, u32[]{:S(2)}) copy-start(s32[32]{0:T(128)} %param.16) | copy-start | bytes 388
  34.9 436.5 %all-gather.5.cloned.1.call-start = ((), (), s32[]{:S(2)}) async-start(), calls=%async_computation.1 | async-start | bytes 28835840 | tf_op jit(solution)/shard_map/all_gather | solution.py:89
  35.6 9.4 %copy-start.7 = (s32[4,2,4]{2,1,0:T(2,128)S(1)}, s32[4,2,4]{2,1,0:T(2,128)}, u32[]{:S(2)}) copy-start(s32[4,2,4]{2,1,0:T(2,128)} %param.19) | copy-start | bytes 388
  35.7 9.6 %copy-start.3 = (f32[4,64,128]{2,1,0:T(8,128)S(1)}, f32[4,64,128]{2,1,0:T(8,128)}, u32[]{:S(2)}) copy-start(f32[4,64,128]{2,1,0:T(8,128)} %param.11) | copy-start | bytes 393220
  35.7 9.6 %copy-start.6 = (s32[4,2,4]{2,1,0:T(2,128)S(1)}, s32[4,2,4]{2,1,0:T(2,128)}, u32[]{:S(2)}) copy-start(s32[4,2,4]{2,1,0:T(2,128)} %param.18) | copy-start | bytes 388
  35.7 9.6 %copy-start.4 = (bf16[88,88]{1,0:T(8,128)(2,1)S(1)}, bf16[88,88]{1,0:T(8,128)(2,1)}, u32[]{:S(2)}) copy-start(bf16[88,88]{1,0:T(8,128)(2,1)} %param.14) | copy-start | bytes 46468
  132.1 351.0 %copy-start.1 = (f32[4,64,128]{2,1,0:T(8,128)S(1)}, f32[4,64,128]{2,1,0:T(8,128)}, u32[]{:S(2)}) copy-start(f32[4,64,128]{2,1,0:T(8,128)} %param.13) | copy-start | bytes 393220
  132.1 351.0 %copy-start.2 = (f32[4,64,128]{2,1,0:T(8,128)S(1)}, f32[4,64,128]{2,1,0:T(8,128)}, u32[]{:S(2)}) copy-start(f32[4,64,128]{2,1,0:T(8,128)} %param.12) | copy-start | bytes 393220
Sparse Core Ops, SparseCore 0:
  35.0 43.6 all-gather.2
  80.3 391.0 all-gather.4
where the time goes:
time: 583 us
  waiting for transfers between devices  362 us (62%)
  other arithmetic  115 us (20%)
  local copies, waits for them, and re-layouts  69.1 us (12%)
  matrix products  23 us (4%)
  between operations  13.6 us (2%)
    all_gather x1, waiting for transfers between devices, body(): lax.all_gather(state, 'line', axis=2, tiled=True)  339 us
    convert_element_type x1, other arithmetic, section_update(): return (smooth + section_step * residual).astype(jnp.bfloat16)  92.7 us
    all_gather x1, waiting for transfers between devices, body(): gathered = lax.all_gather(edge_cells(state), 'blk', axis=0, tiled=True)  22.2 us
    transpose x1, local copies, waits for them, and re-layouts, select_ghosts(): picked = jnp.transpose(picked, (0, 1, 3, 2, 4, 5))  19.2 us
    rev x1, local copies, waits for them, and re-layouts, section_update(): jnp.flip(ghosts[:, 0].astype(jnp.float32), -1)  17.6 us
    unnamed x20, local copies, waits for them, and re-layouts  16.4 us
    convert_element_type x1, other arithmetic, section_update(): ghosts[:, 0].astype(jnp.float32)  12.3 us
    dot_general x1, matrix products, body(): jnp.einsum('lm,bcmp->bclp', my_rows, lax.all_gather(state, 'line', axis=2...  11.7 us
  transfers between devices with their start and end apart: 2, of which 2 were waited for; matrix products, arithmetic and copies ran while one was open for 13% of the time, Pallas kernels for 0%

commit v1 on v0

v1 whole, which is shorter than its diff:
```python
import math

import jax
import jax.numpy as jnp
import numpy as np
from jax import lax
from jax.experimental import pallas as pl
from jax.experimental.pallas import tpu as pltpu
from jax.sharding import PartitionSpec as P


filter_sigma = 0.5
section_step = 0.25
deriv_coef = [5.0 / 6.0, -5.0 / 21.0, 5.0 / 84.0, -5.0 / 504.0, 1.0 / 1260.0]
high_pass = [(-1) ** offset * math.comb(10, 5 + offset) / 1024.0 for offset in range(-5, 6)]
DEPTH = 5
SUB = 8
bf16 = jnp.bfloat16
f32 = jnp.float32


def source_faces(block_perm, patch_src, patch_wall, first_slot):
    nblocks = block_perm.shape[0]
    block_ids = jnp.arange(nblocks, dtype=jnp.int32)
    matches = block_perm[None, :] == block_ids[:, None]
    slot_of = jnp.sum(jnp.where(matches, block_ids[None, :], 0), axis=1)
    owned = patch_src.shape[0]
    own_face = (first_slot + jnp.arange(owned, dtype=jnp.int32))[:, None, None] * 2 + jnp.arange(
        2, dtype=jnp.int32
    )[None, :, None]
    remote = jnp.take(slot_of, patch_src // 2) * 2 + patch_src % 2
    return jnp.where(patch_wall == 1, own_face, remote)


def face_selector(columns):
    pick = np.zeros((2 * SUB, columns), np.float32)
    for d in range(DEPTH):
        pick[d, d] = 1.0
        pick[SUB + d, columns - 1 - d] = 1.0
    return pick


def ghost_placer(columns):
    place = np.zeros((2 * SUB, columns), np.float32)
    for d in range(DEPTH):
        place[d, columns - 1 - d] = 1.0
        place[SUB + d, d] = 1.0
    return place


def flip_pair(size, group):
    same = np.eye(size, dtype=np.float32)
    turned = np.zeros((size, size), np.float32)
    for lane in range(size):
        turned[lane, lane // group * group + group - 1 - lane % group] = 1.0
    return np.stack([same, turned])


def pack_strips(state, patches):
    owned, chans, rows, columns = state.shape
    per = rows // patches
    wide = chans * per

    def kernel(pick_ref, x_ref, *refs):
        o_ref = refs[-1]
        for k in range(patches):
            cells = x_ref[0, :, k * per : (k + 1) * per, :].reshape(wide, columns)
            strip = lax.dot_general(
                pick_ref[...], cells, (((1,), (1,)), ((), ())), preferred_element_type=f32
            ).astype(bf16)
            o_ref[0, 0, k] = strip[:SUB]
            o_ref[0, 1, k] = strip[SUB:]

    return pl.pallas_call(
        kernel,
        grid=(owned,),
        in_specs=[
            pl.BlockSpec((2 * SUB, columns), lambda s: (0, 0)),
            pl.BlockSpec((1, chans, rows, columns), lambda s: (s, 0, 0, 0)),
        ],
        out_specs=pl.BlockSpec((1, 2, patches, SUB, wide), lambda s: (s, 0, 0, 0, 0)),
        out_shape=jax.ShapeDtypeStruct((owned, 2, patches, SUB, wide), bf16),
        cost_estimate=pl.CostEstimate(
            flops=2 * 2 * SUB * state.size, bytes_accessed=3 * state.size, transcendentals=0
        ),
        name="pack_strips",
    )(jnp.asarray(face_selector(columns), bf16), state)


def pick_groups(me, groups, first, count, block):
    n, _, rows, columns = groups.shape

    def kernel(me_ref, *refs):
        for j in range(n - 1):
            refs[n - 1 + j][...] = refs[j][0]

    def chosen(j):
        return lambda i, me: (lax.rem(me[0] + j, n), first // block + i, 0, 0)

    size = (n - 1) * count * rows * columns
    return pl.pallas_call(
        kernel,
        grid_spec=pltpu.PrefetchScalarGridSpec(
            num_scalar_prefetch=1,
            grid=(count // block,),
            in_specs=[pl.BlockSpec((1, block, rows, columns), chosen(j)) for j in range(1, n)],
            out_specs=[pl.BlockSpec((block, rows, columns), lambda i, me: (i, 0, 0))] * (n - 1),
        ),
        out_shape=[jax.ShapeDtypeStruct((count, rows, columns), groups.dtype)] * (n - 1),
        cost_estimate=pl.CostEstimate(flops=0, bytes_accessed=4 * size, transcendentals=0),
        name="pick_groups",
    )(me, *[groups] * (n - 1))


def local_part(state, mixed, speed_in, density, strips, source, flips):
    owned, chans, rows, columns = state.shape
    patches = strips.shape[1]
    per = rows // patches
    wide = chans * per
    step = columns // per

    def kernel(src_ref, flip_ref, turn_ref, place_ref, x_ref, m_ref, in_ref, den_ref, g0_ref, g1_ref, *refs):
        o_ref = refs[-1]
        s, k = pl.program_id(0), pl.program_id(1)

        def turned(ref, face):
            block = ref[0, 0].astype(f32)
            stacked = jnp.concatenate(
                [block[:, i * columns : (i + 1) * columns] for i in range(wide // columns)], 0
            ).astype(bf16)
            turn = turn_ref[flip_ref[(s * 2 + face) * patches + k]]
            return jnp.dot(stacked, turn, preferred_element_type=f32)

        low, high = turned(g0_ref, 0), turned(g1_ref, 1)
        lane = lax.broadcasted_iota(jnp.int32, (step * per, columns), 1)
        speed = jnp.broadcast_to(-section_step * in_ref[...], (step, per, columns)).reshape(-1, columns)
        dens = jnp.broadcast_to(section_step * den_ref[...], (step, per, columns)).reshape(-1, columns)
        for i in range(chans // step):
            both = jnp.concatenate([low[i * SUB : (i + 1) * SUB], high[i * SUB : (i + 1) * SUB]], 0)
            ghost = lax.dot_general(
                both.astype(bf16), place_ref[...], (((0,), (0,)), ((), ())), preferred_element_type=f32
            )
            x = x_ref[0, i * step : (i + 1) * step].reshape(step * per, columns).astype(f32)
            smooth = (1.0 - filter_sigma * high_pass[5]) * x
            slope = jnp.zeros_like(x)
            for j in range(1, DEPTH + 1):
                after = pltpu.roll(jnp.where(lane < j, ghost, x), columns - j, 1)
                before = pltpu.roll(jnp.where(lane >= columns - j, ghost, x), j, 1)
                smooth = smooth - (filter_sigma * high_pass[5 + j]) * (after + before)
                slope = slope + deriv_coef[j - 1] * (after - before)
            mix = m_ref[0, i * step : (i + 1) * step].reshape(step * per, columns)
            base = smooth + speed * slope + dens * mix
            o_ref[0, i * step : (i + 1) * step] = base.reshape(step, per, columns)

    def cells(s, k, *_):
        return (s, 0, k, 0)

    def line(s, k, *_):
        return (s, k, 0)

    def ghosts(face):
        return lambda s, k, src, flip: (src[(s * 2 + face) * patches + k], k, 0, 0)

    return pl.pallas_call(
        kernel,
        grid_spec=pltpu.PrefetchScalarGridSpec(
            num_scalar_prefetch=2,
            grid=(owned, patches),
            in_specs=[
                pl.BlockSpec((2, columns, columns), lambda s, k, *_: (0, 0, 0)),
                pl.BlockSpec((2 * SUB, columns), lambda s, k, *_: (0, 0)),
                pl.BlockSpec((1, chans, per, columns), cells),
                pl.BlockSpec((1, chans, per, columns), cells),
                pl.BlockSpec((1, per, columns), line),
                pl.BlockSpec((1, per, columns), line),
                pl.BlockSpec((1, 1, SUB, wide), ghosts(0)),
                pl.BlockSpec((1, 1, SUB, wide), ghosts(1)),
            ],
            out_specs=pl.BlockSpec((1, chans, per, columns), cells),
        ),
        out_shape=jax.ShapeDtypeStruct(state.shape, f32),
        cost_estimate=pl.CostEstimate(
            flops=60 * state.size, bytes_accessed=10 * state.size, transcendentals=0
        ),
        name="local_part",
    )(
        source.reshape(-1),
        flips.reshape(-1),
        jnp.asarray(flip_pair(columns, per), bf16),
        jnp.asarray(ghost_placer(columns), bf16),
        state,
        mixed,
        speed_in,
        density,
        strips,
        strips,
    )


def wall_product(me, groups, operator, arrived, first, block):
    n, _, rows, columns = groups.shape
    count = arrived[0].shape[0]

    def kernel(me_ref, w_ref, own_ref, *refs):
        ins, outs = refs[: n - 1], refs[-n:]
        lines = []
        for i in range(block):
            lines.append(jnp.concatenate([own_ref[0, i]] + [ref[i] for ref in ins], 0))
        whole = jnp.dot(w_ref[...], jnp.concatenate(lines, 1), preferred_element_type=f32).astype(bf16)
        for j in range(n):
            for i in range(block):
                outs[j][i] = whole[j * rows : (j + 1) * rows, i * columns : (i + 1) * columns]

    piece = pl.BlockSpec((block, rows, columns), lambda i, me: (i, 0, 0))
    size = n * count * rows * columns
    return pl.pallas_call(
        kernel,
        grid_spec=pltpu.PrefetchScalarGridSpec(
            num_scalar_prefetch=1,
            grid=(count // block,),
            in_specs=[
                pl.BlockSpec((n * rows, n * rows), lambda i, me: (0, 0)),
                pl.BlockSpec((1, block, rows, columns), lambda i, me: (me[0], first // block + i, 0, 0)),
            ]
            + [piece] * (n - 1),
            out_specs=[piece] * n,
        ),
        out_shape=[jax.ShapeDtypeStruct((count, rows, columns), bf16)] * n,
        cost_estimate=pl.CostEstimate(
            flops=2 * n * rows * size, bytes_accessed=4 * size, transcendentals=0
        ),
        name="wall_product",
    )(me, operator, groups, *arrived)


def finish(me, base, speed_wall, normals, out, first, block):
    n, _, rows, columns = base.shape
    count = normals[0].shape[0]
    per_slot = n // speed_wall.shape[0]
    fresh = out is None

    def kernel(me_ref, speed_ref, base_ref, *refs):
        o_ref = refs[-1]
        for j in range(n):
            group = lax.rem(me_ref[0] + (n - j), n)
            speed = -section_step * speed_ref[group // per_slot]
            o_ref[group] = (base_ref[group] + speed[None] * refs[j][...].astype(f32)).astype(bf16)

    whole = pl.BlockSpec((n, block, rows, columns), lambda i, me: (0, first // block + i, 0, 0))
    size = n * count * rows * columns
    return pl.pallas_call(
        kernel,
        grid_spec=pltpu.PrefetchScalarGridSpec(
            num_scalar_prefetch=1,
            grid=(count // block,),
            in_specs=[pl.BlockSpec(speed_wall.shape, lambda i, me: (0, 0, 0)), whole]
            + [pl.BlockSpec((block, rows, columns), lambda i, me: (i, 0, 0))] * n
            + [pl.BlockSpec(memory_space=pl.ANY)] * (not fresh),
            out_specs=whole,
        ),
        out_shape=jax.ShapeDtypeStruct(base.shape, bf16),
        input_output_aliases={} if fresh else {3 + n: 0},
        cost_estimate=pl.CostEstimate(flops=2 * size, bytes_accessed=8 * size, transcendentals=0),
        name="finish",
    )(me, speed_wall, base, *normals, *([] if fresh else [out]))


def chunk_blocks(blocks):
    if blocks < 4:
        return [1] * blocks
    middle = (blocks - 2) // 2
    return [1, middle, blocks - 2 - middle, 1]


def sizes(n, owned, chans):
    items = owned * chans // n
    return items, max(size for size in range(1, 12) if items % size == 0 and (size == 8 or items % 8))


def body(n, nblk, state, speed_in, speed_wall, density, rates, wall_op, block_perm, patch_src, patch_flip, patch_wall):
    owned, chans, rows, columns = state.shape
    patches = patch_src.shape[2]
    me = lax.axis_index("line")
    mine = lax.axis_index("blk")
    items, block = sizes(n, owned, chans)
    groups = state.reshape(n, items, rows, columns)
    where = me.astype(jnp.int32).reshape(1)
    shifts = [[(i, (i + j) % n) for i in range(n)] for j in range(n)]

    chunks, first = [], 0
    for size in chunk_blocks(items // block):
        chunks.append((first, size * block))
        first += size * block

    def send(pieces):
        came = []
        for j in range(1, n):
            came.append(lax.ppermute(pieces[j - 1], "line", shifts[j]))
        return came

    arrived = []
    for first, count in chunks:
        picked = pick_groups(where, groups, first, count, block)
        arrived.append(send(picked))

    strips = pack_strips(state, patches)
    gathered = [strips]
    for r in range(1, nblk):
        gathered.append(lax.ppermute(strips, "blk", [(i, i ^ r) for i in range(nblk)]))
    gathered = jnp.concatenate(gathered, 0).reshape((nblk * owned * 2,) + strips.shape[2:])
    source = source_faces(block_perm, patch_src, patch_wall, mine * owned)
    per_device = 2 * owned
    held = ((source // per_device) ^ mine) * per_device + source % per_device

    tiles = wall_op.reshape(n, rows, n, rows)[:, :, ::-1]
    tiles = jnp.concatenate([tiles, tiles], 0)
    tiles = lax.dynamic_slice_in_dim(tiles, me, n, 0)
    tiles = jnp.concatenate([tiles, tiles], 2)
    operator = lax.dynamic_slice_in_dim(tiles, n - 1 - me, n, 2).reshape(n * rows, n * rows)

    mixed = jnp.einsum("ce,belp->bclp", rates, state, preferred_element_type=f32)

    base = local_part(state, mixed, speed_in, density, gathered, held.astype(jnp.int32), patch_flip)
    base = base.reshape(n, items, rows, columns)

    returned = []
    for (first, count), came in zip(chunks, arrived):
        products = wall_product(where, groups, operator, came, first, block)
        returned.append([products[0]] + send(products[1:]))
    out = None
    for (first, count), normals in zip(chunks, returned):
        out = finish(where, base, speed_wall, normals, out, first, block)
    return out.reshape(state.shape)


def solution(mesh):
    n, nblk = mesh.shape["line"], mesh.shape["blk"]

    def section(*args):
        return body(n, nblk, *args)

    return jax.shard_map(
        section,
        mesh=mesh,
        in_specs=(
            P("blk", None, "line", None),
            P("blk", "line", None),
            P("blk", "line", None),
            P("blk", "line", None),
            P(),
            P(),
            P(),
            P("blk", None, "line"),
            P("blk", None, "line"),
            P("blk", None, "line"),
        ),
        out_specs=P("blk", None, "line", None),
        check_vma=False,
    )
```

time: 583 us -> 355 us (0.61)
  the two profiles are of different devices: /device:TPU:0 before, /device:TPU:30 now
where the time goes in v1:
time: 355 us; the launch traced here: 354 us
  starting transfers between devices  123 us (35%)
  waiting for transfers between devices  104 us (29%)
  Pallas kernels  89.9 us (25%)
  local copies, waits for them, and re-layouts  24.5 us (7%)
  matrix products  11.1 us (3%)
    ppermute x24, starting transfers between devices, send(): came.append(lax.ppermute(pieces[j - 1], 'line', shifts[j]))  117 us
    ppermute x24, waiting for transfers between devices, send(): came.append(lax.ppermute(pieces[j - 1], 'line', shifts[j]))  56.5 us
    ppermute x7, waiting for transfers between devices, body(): lax.ppermute(strips, 'blk', [(i, i ^ r) for i in range(nblk)])  47.1 us
    pallas_call x1, Pallas kernels, local_part(): pl.pallas_call(kernel, grid_spec=pltpu.PrefetchScalarGridSpec(num_scalar_...  42.4 us
    pallas_call x4, Pallas kernels, finish(): pl.pallas_call(kernel, grid_spec=pltpu.PrefetchScalarGridSpec(num_scalar_...  15.9 us
    pallas_call x4, Pallas kernels, wall_product(): pl.pallas_call(kernel, grid_spec=pltpu.PrefetchScalarGridSpec(num_scalar_...  14.6 us
    pallas_call x4, Pallas kernels, pick_groups(): pl.pallas_call(kernel, grid_spec=pltpu.PrefetchScalarGridSpec(num_scalar_...  11.8 us
    dot_general x1, matrix products, body(): jnp.einsum('ce,belp->bclp', rates, state, preferred_element_type=f32)  11.1 us
  transfers between devices with their start and end apart: 31, of which 5 were waited for; matrix products, arithmetic and copies ran while one was open for 10% of the time, Pallas kernels for 24%

profile of v1, /device:TPU:30, one launch (start us, length us, event | category | flops | bytes accessed | tf_op | source)
XLA Modules:
  0.0 353.9 jit_solution(7132134186012801527)
XLA Ops:
  0.0 1.8 pick_groups.4
  1.8 0.2 collective-permute-start.7
  2.0 3.6 %pick_groups.6 = (bf16[32,64,128]{2,1,0:T(8,128)(2,1)}, bf16[32,64,128]{2,1,0:T(8,128)(2,1)}, bf16[32,64,128]{2,1,0:T(8,128)(2,1)}) custom-call(s32[1]{0:T(128)} %bitcast.me_ref, bf16[4,88,64,128]{3,2,1,0:T(8,128)(2,1)} %own_ref.7, bf16[4,88,64,128]{3,2,1,0:T(8,128)(2,1)} %own_ref.7, bf16[4,88,64,128]{3,2,1,0:T(8,128)(2,1)} %own_ref.7), custom_call_target="tpu_custom_call" | custom-call | bytes 3145728 | tf_op jit(solution)/shard_map/pick_groups/pallas_call | solution.py:101
  5.7 1.6 collective-permute-start.19
  7.2 1.8 pick_groups.7
  9.0 1.6 collective-permute-start.25
  10.6 0.3 collective-permute-start.26
  10.9 1.8 collective-permute-start.27
  12.7 11.1 %fusion = f32[4,64,128,88]{2,3,1,0:T(8,128)} fusion(bf16[4,88,64,128]{3,2,1,0:T(8,128)(2,1)} %own_ref.7, bf16[88,88]{1,0:T(8,128)(2,1)S(1)} %copy-done), kind=kOutput, calls=%fused_computation.2 | convolution fusion | flops 507510784 | bytes 17316992 | tf_op jit(solution)/shard_map/ce,belp->bclp/dot_general | solution.py:321
  24.0 0.5 rev.3
  24.6 0.4 fusion.3
  25.0 4.6 %pick_groups.5 = (bf16[40,64,128]{2,1,0:T(8,128)(2,1)}, bf16[40,64,128]{2,1,0:T(8,128)(2,1)}, bf16[40,64,128]{2,1,0:T(8,128)(2,1)}) custom-call(s32[1]{0:T(128)} %bitcast.me_ref, bf16[4,88,64,128]{3,2,1,0:T(8,128)(2,1)} %own_ref.7, bf16[4,88,64,128]{3,2,1,0:T(8,128)(2,1)} %own_ref.7, bf16[4,88,64,128]{3,2,1,0:T(8,128)(2,1)} %own_ref.7), custom_call_target="tpu_custom_call" | custom-call | bytes 3932160 | tf_op jit(solution)/shard_map/pick_groups/pallas_call | solution.py:101
  29.6 1.3 collective-permute-start.8
  30.9 0.6 fusion.2
  31.5 0.9 reshape.59.w_ref
  32.4 1.4 collective-permute-start.9
  33.8 2.5 collective-permute-start.13
  36.3 2.2 wall_product.7
  38.6 2.5 collective-permute-done.8.refs_1_
  41.2 0.6 collective-permute-start.28
  41.8 26.7 %collective-permute-start.21 = (bf16[32,64,128]{2,1,0:T(8,128)(2,1)S(1)}, bf16[32,64,128]{2,1,0:T(8,128)(2,1)}, u32[]{:S(2)}, u32[]{:S(2)}) collective-permute-start(bf16[32,64,128]{2,1,0:T(8,128)(2,1)S(1)} %copy-done.23), channel_id=1, source_target_pairs={{0,3},{1,0},{2,1},{3,2},{4,7},{5,4},{6,5},{7,6},{8,11},{9,8},{10,9... | collective-permute-start | bytes 1572872 | tf_op jit(solution)/shard_map/ppermute | solution.py:298
  68.7 5.3 %pack_strips.1 = bf16[4,2,4,8,1408]{4,3,2,1,0:T(8,128)(2,1)} custom-call(bf16[16,128]{1,0:T(8,128)(2,1)} %constant.86.clone.pick_ref, bf16[4,88,64,128]{3,2,1,0:T(8,128)(2,1)} %own_ref.7), custom_call_target="tpu_custom_call" | custom-call | flops 92274688 | bytes 8650752 | tf_op jit(solution)/shard_map/pack_strips/pallas_call | solution.py:74
  74.0 16.6 %collective-permute-start.14 = (bf16[40,64,128]{2,1,0:T(8,128)(2,1)}, bf16[40,64,128]{2,1,0:T(8,128)(2,1)}, u32[]{:S(2)}, u32[]{:S(2)}) collective-permute-start(bf16[40,64,128]{2,1,0:T(8,128)(2,1)} %get-tuple-element.41), channel_id=1, source_target_pairs={{0,2},{1,3},{2,0},{3,1},{4,6},{5,7},{6,4},{7,5},{8,10},{9,11},{10,... | collective-permute-start | bytes 1966088 | tf_op jit(solution)/shard_map/ppermute | solution.py:298
  90.6 1.0 collective-permute-start.15
  91.5 2.0 constant_dynamic-update-slice_fusion.7
  93.7 0.7 gather_fusion
  94.5 0.6 collective-permute-start.1
  95.1 1.3 collective-permute-start.2
  96.5 39.3 %collective-permute-done.14.refs_1_ = bf16[40,64,128]{2,1,0:T(8,128)(2,1)} collective-permute-done((bf16[40,64,128]{2,1,0:T(8,128)(2,1)}, bf16[40,64,128]{2,1,0:T(8,128)(2,1)}, u32[]{:S(2)}, u32[]{:S(2)}) %collective-permute-start.14) | collective-permute-done | bytes 655392 | tf_op jit(solution)/shard_map/ppermute | solution.py:298
  135.9 0.7 reshape.55.src_ref
  136.5 0.6 reshape.56.flip_ref
  137.1 10.5 %copy.27 = f32[4,64,128,88]{2,1,3,0:T(8,128)} copy(f32[4,64,128,88]{2,3,1,0:T(8,128)} %fusion) | data formatting | bytes 23068672 | tf_op jit(solution)/shard_map/ce,belp->bclp/dot_general | solution.py:321
  147.7 2.2 wall_product.4
  149.9 4.5 %wall_product.6 = (bf16[32,64,128]{2,1,0:T(8,128)(2,1)}, bf16[32,64,128]{2,1,0:T(8,128)(2,1)}, bf16[32,64,128]{2,1,0:T(8,128)(2,1)}, bf16[32,64,128]{2,1,0:T(8,128)(2,1)}) custom-call(s32[1]{0:T(128)} %bitcast.me_ref, bf16[256,256]{1,0:T(8,128)(2,1)} %reshape.59.w_ref, bf16[4,88,64,128]{3,2,1,0:T(8,128)(2,1)} %own_ref.7, bf16[32,64,128]{2,1,0:T(8,128)(2,1)} %copy-done.7, ...), custom_call_target="tpu_custom_call" | custom-call | flops 536870912 | bytes 4194304 | tf_op jit(solution)/shard_map/wall_product/pallas_call | solution.py:216
  154.4 5.6 %wall_product.5 = (bf16[40,64,128]{2,1,0:T(8,128)(2,1)}, bf16[40,64,128]{2,1,0:T(8,128)(2,1)}, bf16[40,64,128]{2,1,0:T(8,128)(2,1)}, bf16[40,64,128]{2,1,0:T(8,128)(2,1)}) custom-call(s32[1]{0:T(128)} %bitcast.me_ref, bf16[256,256]{1,0:T(8,128)(2,1)} %reshape.59.w_ref, bf16[4,88,64,128]{3,2,1,0:T(8,128)(2,1)} %own_ref.7, bf16[40,64,128]{2,1,0:T(8,128)(2,1)} %copy-done.6, ...), custom_call_target="tpu_custom_call" | custom-call | flops 671088640 | bytes 5242880 | tf_op jit(solution)/shard_map/wall_product/pallas_call | solution.py:216
  160.0 0.6 collective-permute-start.3
  160.6 1.6 collective-permute-start.5
  162.1 0.9 constant_dynamic-update-slice_fusion.6
  163.1 2.3 collective-permute-start.6
  165.4 3.8 %collective-permute-start.22 = (bf16[32,64,128]{2,1,0:T(8,128)(2,1)}, bf16[32,64,128]{2,1,0:T(8,128)(2,1)S(1)}, u32[]{:S(2)}, u32[]{:S(2)}) collective-permute-start(bf16[32,64,128]{2,1,0:T(8,128)(2,1)} %get-tuple-element.51), channel_id=1, source_target_pairs={{0,1},{1,2},{2,3},{3,0},{4,5},{5,6},{6,7},{7,4},{8,9},{9,10},{10,1... | collective-permute-start | bytes 1572872 | tf_op jit(solution)/shard_map/ppermute | solution.py:298
  169.2 0.9 constant_dynamic-update-slice_fusion.5
  170.1 0.9 constant_dynamic-update-slice_fusion.4
  171.0 38.9 %collective-permute-done.3 = bf16[4,2,4,8,1408]{4,3,2,1,0:T(8,128)(2,1)S(1)} collective-permute-done((bf16[4,2,4,8,1408]{4,3,2,1,0:T(8,128)(2,1)S(1)}, bf16[4,2,4,8,1408]{4,3,2,1,0:T(8,128)(2,1)S(1)}, u32[]{:S(2)}, u32[]{:S(2)}) %collective-permute-start.3) | collective-permute-done | bytes 720928 | tf_op jit(solution)/shard_map/ppermute | solution.py:309
  210.0 2.9 collective-permute-start.23
  212.9 8.1 %collective-permute-done.4 = bf16[4,2,4,8,1408]{4,3,2,1,0:T(8,128)(2,1)S(1)} collective-permute-done((bf16[4,2,4,8,1408]{4,3,2,1,0:T(8,128)(2,1)S(1)}, bf16[4,2,4,8,1408]{4,3,2,1,0:T(8,128)(2,1)S(1)}, u32[]{:S(2)}, u32[]{:S(2)}) %collective-permute-start.4) | collective-permute-done | bytes 720928 | tf_op jit(solution)/shard_map/ppermute | solution.py:309
  221.0 2.9 collective-permute-start.24
  223.9 0.9 collective-permute-start.16
  224.8 0.9 constant_dynamic-update-slice_fusion.3
  225.7 0.8 collective-permute-start.17
  226.6 1.5 collective-permute-start.18
  228.0 0.9 constant_dynamic-update-slice_fusion.2
  229.0 0.9 constant_dynamic-update-slice_fusion.1
  229.9 14.6 %collective-permute-done.23.refs_2_ = bf16[32,64,128]{2,1,0:T(8,128)(2,1)S(1)} collective-permute-done((bf16[32,64,128]{2,1,0:T(8,128)(2,1)}, bf16[32,64,128]{2,1,0:T(8,128)(2,1)S(1)}, u32[]{:S(2)}, u32[]{:S(2)}) %collective-permute-start.23) | collective-permute-done | bytes 524320 | tf_op jit(solution)/shard_map/ppermute | solution.py:298
  244.5 29.2 %collective-permute-start.11 = (bf16[8,64,128]{2,1,0:T(8,128)(2,1)}, bf16[8,64,128]{2,1,0:T(8,128)(2,1)}, u32[]{:S(2)}, u32[]{:S(2)}) collective-permute-start(bf16[8,64,128]{2,1,0:T(8,128)(2,1)} %get-tuple-element.38), channel_id=1, source_target_pairs={{0,2},{1,3},{2,0},{3,1},{4,6},{5,7},{6,4},{7,5},{8,10},{9,11},{10,... | collective-permute-start | bytes 393224 | tf_op jit(solution)/shard_map/ppermute | solution.py:298
  273.8 19.1 %collective-permute-start.12 = (bf16[8,64,128]{2,1,0:T(8,128)(2,1)}, bf16[8,64,128]{2,1,0:T(8,128)(2,1)}, u32[]{:S(2)}, u32[]{:S(2)}) collective-permute-start(bf16[8,64,128]{2,1,0:T(8,128)(2,1)} %get-tuple-element.39), channel_id=1, source_target_pairs={{0,3},{1,0},{2,1},{3,2},{4,7},{5,4},{6,5},{7,6},{8,11},{9,8},{10,9... | collective-permute-start | bytes 393224 | tf_op jit(solution)/shard_map/ppermute | solution.py:298
  292.8 0.9 constant_dynamic-update-slice_fusion
  293.8 42.4 %local_part.1.base_ref = f32[4,88,64,128]{3,2,1,0:T(8,128)} custom-call(s32[32]{0:T(128)} %reshape.55.src_ref, s32[32]{0:T(128)} %reshape.56.flip_ref, bf16[2,128,128]{2,1,0:T(8,128)(2,1)} %constant.87.clone.turn_ref, bf16[16,128]{1,0:T(8,128)(2,1)} %constant.88.clone.place_ref, bf16[4,88,64,128]{3,2,1,0:T(8,128)(2,1)} %own_ref.7, ...), custom_call_target="tpu_custom_call" | custom-call | flops 173015040 | bytes 28835840 | tf_op jit(solution)/shard_map/local_part/pallas_call | solution.py:164
  336.1 2.4 finish.4.refs_4_
  338.5 4.8 %finish.5.refs_4_ = bf16[4,88,64,128]{3,2,1,0:T(8,128)(2,1)} custom-call(s32[1]{0:T(128)} %bitcast.me_ref, f32[4,64,128]{2,1,0:T(8,128)} %speed_ref.7, f32[4,88,64,128]{3,2,1,0:T(8,128)} %local_part.1.base_ref, bf16[32,64,128]{2,1,0:T(8,128)(2,1)} %get-tuple-element.50.refs_0_, bf16[32,64,128]{2,1,0:T(8,128)(2,1)} %copy-done.8, ...), custom_call_target="tpu_custom_call", output_to_operand_aliasing={{}: (7, {})} | custom-call | flops 2097152 | bytes 8388608 | tf_op jit(solution)/shard_map/finish/pallas_call | solution.py:251
  343.4 0.8 copy-done.4
  344.2 0.2 copy-done.5
  344.5 6.3 %finish.6.refs_4_ = bf16[4,88,64,128]{3,2,1,0:T(8,128)(2,1)} custom-call(s32[1]{0:T(128)} %bitcast.me_ref, f32[4,64,128]{2,1,0:T(8,128)} %speed_ref.7, f32[4,88,64,128]{3,2,1,0:T(8,128)} %local_part.1.base_ref, bf16[40,64,128]{2,1,0:T(8,128)(2,1)} %get-tuple-element.43.refs_0_, bf16[40,64,128]{2,1,0:T(8,128)(2,1)} %copy-done.3, ...), custom_call_target="tpu_custom_call", output_to_operand_aliasing={{}: (7, {})} | custom-call | flops 2621440 | bytes 10485760 | tf_op jit(solution)/shard_map/finish/pallas_call | solution.py:251
  350.8 0.6 copy-done.11
  351.5 2.4 finish.7
  (94 shorter events, 1.0 us)
Async XLA Ops:
  0.0 12.7 %copy-start = (bf16[88,88]{1,0:T(8,128)(2,1)S(1)}, bf16[88,88]{1,0:T(8,128)(2,1)}, u32[]{:S(2)}) copy-start(bf16[88,88]{1,0:T(8,128)(2,1)} %param.17) | copy-start | bytes 46468
  1.8 36.7 %collective-permute-start.7 = (bf16[8,64,128]{2,1,0:T(8,128)(2,1)}, bf16[8,64,128]{2,1,0:T(8,128)(2,1)S(1)}, u32[]{:S(2)}, u32[]{:S(2)}) collective-permute-start(bf16[8,64,128]{2,1,0:T(8,128)(2,1)} %get-tuple-element.33), channel_id=1, source_target_pairs={{0,1},{1,2},{2,3},{3,0},{4,5},{5,6},{6,7},{7,4},{8,9},{9,10},{10,1... | collective-permute-start | bytes 393224 | tf_op jit(solution)/shard_map/ppermute | solution.py:298
  5.7 84.9 %collective-permute-start.19 = (bf16[32,64,128]{2,1,0:T(8,128)(2,1)}, bf16[32,64,128]{2,1,0:T(8,128)(2,1)S(1)}, u32[]{:S(2)}, u32[]{:S(2)}) collective-permute-start(bf16[32,64,128]{2,1,0:T(8,128)(2,1)} %get-tuple-element.47), channel_id=1, source_target_pairs={{0,1},{1,2},{2,3},{3,0},{4,5},{5,6},{6,7},{7,4},{8,9},{9,10},{10,1... | collective-permute-start | bytes 1572872 | tf_op jit(solution)/shard_map/ppermute | solution.py:298
  9.0 20.6 %collective-permute-start.25 = (bf16[8,64,128]{2,1,0:T(8,128)(2,1)}, bf16[8,64,128]{2,1,0:T(8,128)(2,1)S(1)}, u32[]{:S(2)}, u32[]{:S(2)}) collective-permute-start(bf16[8,64,128]{2,1,0:T(8,128)(2,1)} %get-tuple-element.54), channel_id=1, source_target_pairs={{0,1},{1,2},{2,3},{3,0},{4,5},{5,6},{6,7},{7,4},{8,9},{9,10},{10,1... | collective-permute-start | bytes 393224 | tf_op jit(solution)/shard_map/ppermute | solution.py:298
  10.6 21.8 %collective-permute-start.26 = (bf16[8,64,128]{2,1,0:T(8,128)(2,1)}, bf16[8,64,128]{2,1,0:T(8,128)(2,1)S(1)}, u32[]{:S(2)}, u32[]{:S(2)}) collective-permute-start(bf16[8,64,128]{2,1,0:T(8,128)(2,1)} %get-tuple-element.55), channel_id=1, source_target_pairs={{0,2},{1,3},{2,0},{3,1},{4,6},{5,7},{6,4},{7,5},{8,10},{9,11},{10,... | collective-permute-start | bytes 393224 | tf_op jit(solution)/shard_map/ppermute | solution.py:298
  10.9 12.9 %copy-start.12 = (bf16[256,256]{1,0:T(8,128)(2,1)S(1)}, bf16[256,256]{1,0:T(8,128)(2,1)}, u32[]{:S(2)}) copy-start(bf16[256,256]{1,0:T(8,128)(2,1)} %param.18) | copy-start | bytes 393220
  10.9 22.9 %collective-permute-start.27 = (bf16[8,64,128]{2,1,0:T(8,128)(2,1)}, bf16[8,64,128]{2,1,0:T(8,128)(2,1)S(1)}, u32[]{:S(2)}, u32[]{:S(2)}) collective-permute-start(bf16[8,64,128]{2,1,0:T(8,128)(2,1)} %get-tuple-element.56), channel_id=1, source_target_pairs={{0,3},{1,0},{2,1},{3,2},{4,7},{5,4},{6,5},{7,6},{8,11},{9,8},{10,9... | collective-permute-start | bytes 393224 | tf_op jit(solution)/shard_map/ppermute | solution.py:298
  25.0 4.6 %copy-start.26 = (bf16[8,64,128]{2,1,0:T(8,128)(2,1)S(1)}, bf16[8,64,128]{2,1,0:T(8,128)(2,1)}, u32[]{:S(2)}) copy-start(bf16[8,64,128]{2,1,0:T(8,128)(2,1)} %get-tuple-element.34) | copy-start | bytes 393220
  25.0 7.4 %copy-start.25 = (bf16[8,64,128]{2,1,0:T(8,128)(2,1)S(1)}, bf16[8,64,128]{2,1,0:T(8,128)(2,1)}, u32[]{:S(2)}) copy-start(bf16[8,64,128]{2,1,0:T(8,128)(2,1)} %get-tuple-element.35) | copy-start | bytes 393220
  29.6 9.0 %copy-start.24 = (bf16[32,64,128]{2,1,0:T(8,128)(2,1)S(1)}, bf16[32,64,128]{2,1,0:T(8,128)(2,1)}, u32[]{:S(2)}) copy-start(bf16[32,64,128]{2,1,0:T(8,128)(2,1)} %get-tuple-element.48) | copy-start | bytes 1572868
  29.6 12.2 %copy-start.20 = (s32[4,2,4]{2,1,0:T(2,128)S(1)}, s32[4,2,4]{2,1,0:T(2,128)}, u32[]{:S(2)}) copy-start(s32[4,2,4]{2,1,0:T(2,128)} %param.20) | copy-start | bytes 388
  29.6 12.2 %copy-start.23 = (bf16[32,64,128]{2,1,0:T(8,128)(2,1)S(1)}, bf16[32,64,128]{2,1,0:T(8,128)(2,1)}, u32[]{:S(2)}) copy-start(bf16[32,64,128]{2,1,0:T(8,128)(2,1)} %get-tuple-element.49) | copy-start | bytes 1572868
  29.6 38.9 %copy-start.27 = (s32[32]{0:T(128)S(1)}, s32[32]{0:T(128)}, u32[]{:S(2)}) copy-start(s32[32]{0:T(128)} %param.19) | copy-start | bytes 388
  29.6 6.7 %copy-start.16 = (bf16[8,64,128]{2,1,0:T(8,128)(2,1)}, bf16[8,64,128]{2,1,0:T(8,128)(2,1)S(1)}, u32[]{:S(2)}) copy-start(bf16[8,64,128]{2,1,0:T(8,128)(2,1)S(1)} %collective-permute-done.25.refs_0_) | copy-start | bytes 393220
  29.6 11.5 %collective-permute-start.8 = (bf16[8,64,128]{2,1,0:T(8,128)(2,1)S(1)}, bf16[8,64,128]{2,1,0:T(8,128)(2,1)S(1)}, u32[]{:S(2)}, u32[]{:S(2)}) collective-permute-start(bf16[8,64,128]{2,1,0:T(8,128)(2,1)S(1)} %copy-done.26), channel_id=1, source_target_pairs={{0,2},{1,3},{2,0},{3,1},{4,6},{5,7},{6,4},{7,5},{8,10},{9,11},{10,... | collective-permute-start | bytes 393224 | tf_op jit(solution)/shard_map/ppermute | solution.py:298
  32.4 3.9 %copy-start.17 = (bf16[8,64,128]{2,1,0:T(8,128)(2,1)}, bf16[8,64,128]{2,1,0:T(8,128)(2,1)S(1)}, u32[]{:S(2)}) copy-start(bf16[8,64,128]{2,1,0:T(8,128)(2,1)S(1)} %collective-permute-done.26.refs_1_) | copy-start | bytes 393220
  32.4 9.4 %collective-permute-start.9 = (bf16[8,64,128]{2,1,0:T(8,128)(2,1)S(1)}, bf16[8,64,128]{2,1,0:T(8,128)(2,1)S(1)}, u32[]{:S(2)}, u32[]{:S(2)}) collective-permute-start(bf16[8,64,128]{2,1,0:T(8,128)(2,1)S(1)} %copy-done.25), channel_id=1, source_target_pairs={{0,3},{1,0},{2,1},{3,2},{4,7},{5,4},{6,5},{7,6},{8,11},{9,8},{10,9... | collective-permute-start | bytes 393224 | tf_op jit(solution)/shard_map/ppermute | solution.py:298
  33.8 2.5 copy-start.18
  33.8 61.3 %collective-permute-start.13 = (bf16[40,64,128]{2,1,0:T(8,128)(2,1)}, bf16[40,64,128]{2,1,0:T(8,128)(2,1)S(1)}, u32[]{:S(2)}, u32[]{:S(2)}) collective-permute-start(bf16[40,64,128]{2,1,0:T(8,128)(2,1)} %get-tuple-element.40), channel_id=1, source_target_pairs={{0,1},{1,2},{2,3},{3,0},{4,5},{5,6},{6,7},{7,4},{8,9},{9,10},{10,1... | collective-permute-start | bytes 1966088 | tf_op jit(solution)/shard_map/ppermute | solution.py:298
  38.5 55.0 %copy-start.13 = (bf16[8,64,128]{2,1,0:T(8,128)(2,1)}, bf16[8,64,128]{2,1,0:T(8,128)(2,1)S(1)}, u32[]{:S(2)}) copy-start(bf16[8,64,128]{2,1,0:T(8,128)(2,1)S(1)} %collective-permute-done.7.refs_0_) | copy-start | bytes 393220
  38.5 55.0 %collective-permute-start.20 = (bf16[32,64,128]{2,1,0:T(8,128)(2,1)S(1)}, bf16[32,64,128]{2,1,0:T(8,128)(2,1)}, u32[]{:S(2)}, u32[]{:S(2)}) collective-permute-start(bf16[32,64,128]{2,1,0:T(8,128)(2,1)S(1)} %copy-done.24), channel_id=1, source_target_pairs={{0,2},{1,3},{2,0},{3,1},{4,6},{5,7},{6,4},{7,5},{8,10},{9,11},{10,... | collective-permute-start | bytes 1572872 | tf_op jit(solution)/shard_map/ppermute | solution.py:298
  41.2 52.4 %copy-start.14 = (bf16[8,64,128]{2,1,0:T(8,128)(2,1)}, bf16[8,64,128]{2,1,0:T(8,128)(2,1)S(1)}, u32[]{:S(2)}) copy-start(bf16[8,64,128]{2,1,0:T(8,128)(2,1)S(1)} %collective-permute-done.8.refs_1_) | copy-start | bytes 393220
  41.2 32.8 %collective-permute-start.28 = (bf16[8,64,128]{2,1,0:T(8,128)(2,1)}, bf16[8,64,128]{2,1,0:T(8,128)(2,1)S(1)}, u32[]{:S(2)}, u32[]{:S(2)}) collective-permute-start(bf16[8,64,128]{2,1,0:T(8,128)(2,1)} %get-tuple-element.58), channel_id=1, source_target_pairs={{0,1},{1,2},{2,3},{3,0},{4,5},{5,6},{6,7},{7,4},{8,9},{9,10},{10,1... | collective-permute-start | bytes 393224 | tf_op jit(solution)/shard_map/ppermute | solution.py:298
  41.8 51.8 %copy-start.15 = (bf16[8,64,128]{2,1,0:T(8,128)(2,1)}, bf16[8,64,128]{2,1,0:T(8,128)(2,1)S(1)}, u32[]{:S(2)}) copy-start(bf16[8,64,128]{2,1,0:T(8,128)(2,1)S(1)} %collective-permute-done.9.refs_2_) | copy-start | bytes 393220
  41.8 52.7 %collective-permute-start.21 = (bf16[32,64,128]{2,1,0:T(8,128)(2,1)S(1)}, bf16[32,64,128]{2,1,0:T(8,128)(2,1)}, u32[]{:S(2)}, u32[]{:S(2)}) collective-permute-start(bf16[32,64,128]{2,1,0:T(8,128)(2,1)S(1)} %copy-done.23), channel_id=1, source_target_pairs={{0,3},{1,0},{2,1},{3,2},{4,7},{5,4},{6,5},{7,6},{8,11},{9,8},{10,9... | collective-permute-start | bytes 1572872 | tf_op jit(solution)/shard_map/ppermute | solution.py:298
  68.7 67.1 %copy-start.21 = (s32[4,2,4]{2,1,0:T(2,128)S(1)}, s32[4,2,4]{2,1,0:T(2,128)}, u32[]{:S(2)}) copy-start(s32[4,2,4]{2,1,0:T(2,128)} %param.22) | copy-start | bytes 388
  68.7 67.9 %copy-start.22 = (s32[4,2,4]{2,1,0:T(2,128)S(1)}, s32[4,2,4]{2,1,0:T(2,128)}, u32[]{:S(2)}) copy-start(s32[4,2,4]{2,1,0:T(2,128)} %param.21) | copy-start | bytes 388
  74.0 19.6 %copy-start.19 = (bf16[8,64,128]{2,1,0:T(8,128)(2,1)}, bf16[8,64,128]{2,1,0:T(8,128)(2,1)S(1)}, u32[]{:S(2)}) copy-start(bf16[8,64,128]{2,1,0:T(8,128)(2,1)S(1)} %collective-permute-done.28.refs_1_) | copy-start | bytes 393220
  74.0 61.8 %collective-permute-start.14 = (bf16[40,64,128]{2,1,0:T(8,128)(2,1)}, bf16[40,64,128]{2,1,0:T(8,128)(2,1)}, u32[]{:S(2)}, u32[]{:S(2)}) collective-permute-start(bf16[40,64,128]{2,1,0:T(8,128)(2,1)} %get-tuple-element.41), channel_id=1, source_target_pairs={{0,2},{1,3},{2,0},{3,1},{4,6},{5,7},{6,4},{7,5},{8,10},{9,11},{10,... | collective-permute-start | bytes 1966088 | tf_op jit(solution)/shard_map/ppermute | solution.py:298
  90.6 57.1 %copy-start.7 = (bf16[32,64,128]{2,1,0:T(8,128)(2,1)}, bf16[32,64,128]{2,1,0:T(8,128)(2,1)S(1)}, u32[]{:S(2)}) copy-start(bf16[32,64,128]{2,1,0:T(8,128)(2,1)S(1)} %collective-permute-done.19.refs_0_) | copy-start | bytes 1572868
  90.6 45.2 %collective-permute-start.15 = (bf16[40,64,128]{2,1,0:T(8,128)(2,1)}, bf16[40,64,128]{2,1,0:T(8,128)(2,1)}, u32[]{:S(2)}, u32[]{:S(2)}) collective-permute-start(bf16[40,64,128]{2,1,0:T(8,128)(2,1)} %get-tuple-element.42), channel_id=1, source_target_pairs={{0,3},{1,0},{2,1},{3,2},{4,7},{5,4},{6,5},{7,6},{8,11},{9,8},{10,9... | collective-permute-start | bytes 1966088 | tf_op jit(solution)/shard_map/ppermute | solution.py:298
  93.6 67.0 %collective-permute-start = (bf16[4,2,4,8,1408]{4,3,2,1,0:T(8,128)(2,1)}, bf16[4,2,4,8,1408]{4,3,2,1,0:T(8,128)(2,1)S(1)}, u32[]{:S(2)}, u32[]{:S(2)}) collective-permute-start(bf16[4,2,4,8,1408]{4,3,2,1,0:T(8,128)(2,1)} %pack_strips.1), channel_id=1, source_target_pairs={{0,4},{4,0},{8,12},{12,8},{16,20},{20,16},{24,28},{28,24},{1,5},{5... | collective-permute-start | bytes 2162696 | tf_op jit(solution)/shard_map/ppermute | solution.py:309
  94.5 68.6 %collective-permute-start.1 = (bf16[4,2,4,8,1408]{4,3,2,1,0:T(8,128)(2,1)}, bf16[4,2,4,8,1408]{4,3,2,1,0:T(8,128)(2,1)S(1)}, u32[]{:S(2)}, u32[]{:S(2)}) collective-permute-start(bf16[4,2,4,8,1408]{4,3,2,1,0:T(8,128)(2,1)} %pack_strips.1), channel_id=1, source_target_pairs={{0,8},{4,12},{8,0},{12,4},{16,24},{20,28},{24,16},{28,20},{1,9},{5... | collective-permute-start | bytes 2162696 | tf_op jit(solution)/shard_map/ppermute | solution.py:309
  95.1 52.6 %copy-start.6 = (bf16[40,64,128]{2,1,0:T(8,128)(2,1)}, bf16[40,64,128]{2,1,0:T(8,128)(2,1)S(1)}, u32[]{:S(2)}) copy-start(bf16[40,64,128]{2,1,0:T(8,128)(2,1)S(1)} %collective-permute-done.13.refs_0_) | copy-start | bytes 1966084
  95.1 70.3 %collective-permute-start.2 = (bf16[4,2,4,8,1408]{4,3,2,1,0:T(8,128)(2,1)}, bf16[4,2,4,8,1408]{4,3,2,1,0:T(8,128)(2,1)S(1)}, u32[]{:S(2)}, u32[]{:S(2)}) collective-permute-start(bf16[4,2,4,8,1408]{4,3,2,1,0:T(8,128)(2,1)} %pack_strips.1), channel_id=1, source_target_pairs={{0,12},{4,8},{8,4},{12,0},{16,28},{20,24},{24,20},{28,16},{1,13},{... | collective-permute-start | bytes 2162696 | tf_op jit(solution)/shard_map/ppermute | solution.py:309
  135.8 24.2 %collective-permute-start.29 = (bf16[8,64,128]{2,1,0:T(8,128)(2,1)}, bf16[8,64,128]{2,1,0:T(8,128)(2,1)}, u32[]{:S(2)}, u32[]{:S(2)}) collective-permute-start(bf16[8,64,128]{2,1,0:T(8,128)(2,1)} %get-tuple-element.59), channel_id=1, source_target_pairs={{0,2},{1,3},{2,0},{3,1},{4,6},{5,7},{6,4},{7,5},{8,10},{9,11},{10,... | collective-permute-start | bytes 393224 | tf_op jit(solution)/shard_map/ppermute | solution.py:298
  135.8 24.8 %collective-permute-start.30 = (bf16[8,64,128]{2,1,0:T(8,128)(2,1)}, bf16[8,64,128]{2,1,0:T(8,128)(2,1)}, u32[]{:S(2)}, u32[]{:S(2)}) collective-permute-start(bf16[8,64,128]{2,1,0:T(8,128)(2,1)} %get-tuple-element.60), channel_id=1, source_target_pairs={{0,3},{1,0},{2,1},{3,2},{4,7},{5,4},{6,5},{7,6},{8,11},{9,8},{10,9... | collective-permute-start | bytes 393224 | tf_op jit(solution)/shard_map/ppermute | solution.py:298
  154.4 5.6 %copy-start.2 = (bf16[4,2,4,8,1408]{4,3,2,1,0:T(8,128)(2,1)S(1)}, bf16[4,2,4,8,1408]{4,3,2,1,0:T(8,128)(2,1)}, u32[]{:S(2)}) copy-start(bf16[4,2,4,8,1408]{4,3,2,1,0:T(8,128)(2,1)} %pack_strips.1) | copy-start | bytes 2162692
  160.0 50.0 %collective-permute-start.3 = (bf16[4,2,4,8,1408]{4,3,2,1,0:T(8,128)(2,1)S(1)}, bf16[4,2,4,8,1408]{4,3,2,1,0:T(8,128)(2,1)S(1)}, u32[]{:S(2)}, u32[]{:S(2)}) collective-permute-start(bf16[4,2,4,8,1408]{4,3,2,1,0:T(8,128)(2,1)S(1)} %copy-done.2), channel_id=1, source_target_pairs={{0,16},{4,20},{8,24},{12,28},{16,0},{20,4},{24,8},{28,12},{1,17},{... | collective-permute-start | bytes 2162696 | tf_op jit(solution)/shard_map/ppermute | solution.py:309
  160.6 60.4 %collective-permute-start.4 = (bf16[4,2,4,8,1408]{4,3,2,1,0:T(8,128)(2,1)S(1)}, bf16[4,2,4,8,1408]{4,3,2,1,0:T(8,128)(2,1)S(1)}, u32[]{:S(2)}, u32[]{:S(2)}) collective-permute-start(bf16[4,2,4,8,1408]{4,3,2,1,0:T(8,128)(2,1)S(1)} %copy-done.2), channel_id=1, source_target_pairs={{0,20},{4,16},{8,28},{12,24},{16,4},{20,0},{24,12},{28,8},{1,21},{... | collective-permute-start | bytes 2162696 | tf_op jit(solution)/shard_map/ppermute | solution.py:309
  160.6 63.3 %collective-permute-start.5 = (bf16[4,2,4,8,1408]{4,3,2,1,0:T(8,128)(2,1)S(1)}, bf16[4,2,4,8,1408]{4,3,2,1,0:T(8,128)(2,1)S(1)}, u32[]{:S(2)}, u32[]{:S(2)}) collective-permute-start(bf16[4,2,4,8,1408]{4,3,2,1,0:T(8,128)(2,1)S(1)} %copy-done.2), channel_id=1, source_target_pairs={{0,24},{4,28},{8,16},{12,20},{16,8},{20,12},{24,0},{28,4},{1,25},{... | collective-permute-start | bytes 2162696 | tf_op jit(solution)/shard_map/ppermute | solution.py:309
  163.1 62.7 %collective-permute-start.6 = (bf16[4,2,4,8,1408]{4,3,2,1,0:T(8,128)(2,1)S(1)}, bf16[4,2,4,8,1408]{4,3,2,1,0:T(8,128)(2,1)S(1)}, u32[]{:S(2)}, u32[]{:S(2)}) collective-permute-start(bf16[4,2,4,8,1408]{4,3,2,1,0:T(8,128)(2,1)S(1)} %copy-done.2), channel_id=1, source_target_pairs={{0,28},{4,24},{8,20},{12,16},{16,12},{20,8},{24,4},{28,0},{1,29},{... | collective-permute-start | bytes 2162696 | tf_op jit(solution)/shard_map/ppermute | solution.py:309
  165.4 61.2 %collective-permute-start.22 = (bf16[32,64,128]{2,1,0:T(8,128)(2,1)}, bf16[32,64,128]{2,1,0:T(8,128)(2,1)S(1)}, u32[]{:S(2)}, u32[]{:S(2)}) collective-permute-start(bf16[32,64,128]{2,1,0:T(8,128)(2,1)} %get-tuple-element.51), channel_id=1, source_target_pairs={{0,1},{1,2},{2,3},{3,0},{4,5},{5,6},{6,7},{7,4},{8,9},{9,10},{10,1... | collective-permute-start | bytes 1572872 | tf_op jit(solution)/shard_map/ppermute | solution.py:298
  210.0 34.6 %collective-permute-start.23 = (bf16[32,64,128]{2,1,0:T(8,128)(2,1)}, bf16[32,64,128]{2,1,0:T(8,128)(2,1)S(1)}, u32[]{:S(2)}, u32[]{:S(2)}) collective-permute-start(bf16[32,64,128]{2,1,0:T(8,128)(2,1)} %get-tuple-element.52), channel_id=1, source_target_pairs={{0,2},{1,3},{2,0},{3,1},{4,6},{5,7},{6,4},{7,5},{8,10},{9,11},{10,... | collective-permute-start | bytes 1572872 | tf_op jit(solution)/shard_map/ppermute | solution.py:298
  221.0 23.5 %collective-permute-start.24 = (bf16[32,64,128]{2,1,0:T(8,128)(2,1)}, bf16[32,64,128]{2,1,0:T(8,128)(2,1)S(1)}, u32[]{:S(2)}, u32[]{:S(2)}) collective-permute-start(bf16[32,64,128]{2,1,0:T(8,128)(2,1)} %get-tuple-element.53), channel_id=1, source_target_pairs={{0,3},{1,0},{2,1},{3,2},{4,7},{5,4},{6,5},{7,6},{8,11},{9,8},{10,9... | collective-permute-start | bytes 1572872 | tf_op jit(solution)/shard_map/ppermute | solution.py:298
  223.9 49.9 %collective-permute-start.16 = (bf16[40,64,128]{2,1,0:T(8,128)(2,1)}, bf16[40,64,128]{2,1,0:T(8,128)(2,1)S(1)}, u32[]{:S(2)}, u32[]{:S(2)}) collective-permute-start(bf16[40,64,128]{2,1,0:T(8,128)(2,1)} %get-tuple-element.44), channel_id=1, source_target_pairs={{0,1},{1,2},{2,3},{3,0},{4,5},{5,6},{6,7},{7,4},{8,9},{9,10},{10,1... | collective-permute-start | bytes 1966088 | tf_op jit(solution)/shard_map/ppermute | solution.py:298
  225.7 117.6 %collective-permute-start.17 = (bf16[40,64,128]{2,1,0:T(8,128)(2,1)}, bf16[40,64,128]{2,1,0:T(8,128)(2,1)S(1)}, u32[]{:S(2)}, u32[]{:S(2)}) collective-permute-start(bf16[40,64,128]{2,1,0:T(8,128)(2,1)} %get-tuple-element.45), channel_id=1, source_target_pairs={{0,2},{1,3},{2,0},{3,1},{4,6},{5,7},{6,4},{7,5},{8,10},{9,11},{10,... | collective-permute-start | bytes 1966088 | tf_op jit(solution)/shard_map/ppermute | solution.py:298
  226.6 109.5 %copy-start.8 = (bf16[32,64,128]{2,1,0:T(8,128)(2,1)}, bf16[32,64,128]{2,1,0:T(8,128)(2,1)S(1)}, u32[]{:S(2)}) copy-start(bf16[32,64,128]{2,1,0:T(8,128)(2,1)S(1)} %collective-permute-done.22.refs_1_) | copy-start | bytes 1572868
  226.6 116.8 %collective-permute-start.18 = (bf16[40,64,128]{2,1,0:T(8,128)(2,1)}, bf16[40,64,128]{2,1,0:T(8,128)(2,1)S(1)}, u32[]{:S(2)}, u32[]{:S(2)}) collective-permute-start(bf16[40,64,128]{2,1,0:T(8,128)(2,1)} %get-tuple-element.46), channel_id=1, source_target_pairs={{0,3},{1,0},{2,1},{3,2},{4,7},{5,4},{6,5},{7,6},{8,11},{9,8},{10,9... | collective-permute-start | bytes 1966088 | tf_op jit(solution)/shard_map/ppermute | solution.py:298
  244.5 49.2 %copy-start.9 = (bf16[32,64,128]{2,1,0:T(8,128)(2,1)}, bf16[32,64,128]{2,1,0:T(8,128)(2,1)S(1)}, u32[]{:S(2)}) copy-start(bf16[32,64,128]{2,1,0:T(8,128)(2,1)S(1)} %collective-permute-done.23.refs_2_) | copy-start | bytes 1572868
  244.5 106.3 %collective-permute-start.10 = (bf16[8,64,128]{2,1,0:T(8,128)(2,1)}, bf16[8,64,128]{2,1,0:T(8,128)(2,1)S(1)}, u32[]{:S(2)}, u32[]{:S(2)}) collective-permute-start(bf16[8,64,128]{2,1,0:T(8,128)(2,1)} %get-tuple-element.37), channel_id=1, source_target_pairs={{0,1},{1,2},{2,3},{3,0},{4,5},{5,6},{6,7},{7,4},{8,9},{9,10},{10,1... | collective-permute-start | bytes 393224 | tf_op jit(solution)/shard_map/ppermute | solution.py:298
  244.5 49.2 %copy-start.10 = (bf16[32,64,128]{2,1,0:T(8,128)(2,1)}, bf16[32,64,128]{2,1,0:T(8,128)(2,1)S(1)}, u32[]{:S(2)}) copy-start(bf16[32,64,128]{2,1,0:T(8,128)(2,1)S(1)} %collective-permute-done.24.refs_3_) | copy-start | bytes 1572868
  244.5 106.3 %collective-permute-start.11 = (bf16[8,64,128]{2,1,0:T(8,128)(2,1)}, bf16[8,64,128]{2,1,0:T(8,128)(2,1)}, u32[]{:S(2)}, u32[]{:S(2)}) collective-permute-start(bf16[8,64,128]{2,1,0:T(8,128)(2,1)} %get-tuple-element.38), channel_id=1, source_target_pairs={{0,2},{1,3},{2,0},{3,1},{4,6},{5,7},{6,4},{7,5},{8,10},{9,11},{10,... | collective-permute-start | bytes 393224 | tf_op jit(solution)/shard_map/ppermute | solution.py:298
  273.8 62.4 %copy-start.3 = (bf16[40,64,128]{2,1,0:T(8,128)(2,1)}, bf16[40,64,128]{2,1,0:T(8,128)(2,1)S(1)}, u32[]{:S(2)}) copy-start(bf16[40,64,128]{2,1,0:T(8,128)(2,1)S(1)} %collective-permute-done.16.refs_1_) | copy-start | bytes 1966084
  273.8 77.1 %collective-permute-start.12 = (bf16[8,64,128]{2,1,0:T(8,128)(2,1)}, bf16[8,64,128]{2,1,0:T(8,128)(2,1)}, u32[]{:S(2)}, u32[]{:S(2)}) collective-permute-start(bf16[8,64,128]{2,1,0:T(8,128)(2,1)} %get-tuple-element.39), channel_id=1, source_target_pairs={{0,3},{1,0},{2,1},{3,2},{4,7},{5,4},{6,5},{7,6},{8,11},{9,8},{10,9... | collective-permute-start | bytes 393224 | tf_op jit(solution)/shard_map/ppermute | solution.py:298
  343.4 0.9 copy-start.4
  343.4 1.1 copy-start.5
  350.8 0.7 copy-start.11
  351.5 2.4 copy-start.1

commit v2 on v1

--- a/solution.py
+++ b/solution.py
@@ -15,6 +15,9 @@
 high_pass = [(-1) ** offset * math.comb(10, 5 + offset) / 1024.0 for offset in range(-5, 6)]
 DEPTH = 5
 SUB = 8
+GRANT = 16 << 20
+FULL_GRANT = 60 << 20
+SCALE = 2520
 bf16 = jnp.bfloat16
 f32 = jnp.float32
 
@@ -40,12 +43,29 @@
     return pick
 
 
-def ghost_placer(columns):
-    place = np.zeros((2 * SUB, columns), np.float32)
-    for d in range(DEPTH):
-        place[d, columns - 1 - d] = 1.0
-        place[SUB + d, d] = 1.0
-    return place
+def bands(columns):
+    weights = np.zeros((3, 2 * DEPTH + 1))
+    for j in range(-DEPTH, DEPTH + 1):
+        weights[0, DEPTH + j] = filter_sigma * high_pass[DEPTH + j]
+        if j:
+            whole = round(deriv_coef[abs(j) - 1] * SCALE)
+            rest = int(math.fmod(whole, 2048)) if abs(whole) > 2048 else 0
+            weights[1, DEPTH + j] = math.copysign(1, j) * (whole - rest)
+            weights[2, DEPTH + j] = math.copysign(1, j) * rest
+    inner = np.zeros((columns, 3 * columns), np.float32)
+    outer = np.zeros((2 * SUB, 3 * columns), np.float32)
+    for band in range(3):
+        for p in range(columns):
+            for j in range(-DEPTH, DEPTH + 1):
+                q = p + j
+                weight = weights[band, DEPTH + j]
+                if q < 0:
+                    outer[-1 - q, band * columns + p] = weight
+                elif q >= columns:
+                    outer[SUB + q - columns, band * columns + p] = weight
+                else:
+                    inner[q, band * columns + p] = weight
+    return inner, outer
 
 
 def flip_pair(size, group):
@@ -83,44 +103,51 @@
         cost_estimate=pl.CostEstimate(
             flops=2 * 2 * SUB * state.size, bytes_accessed=3 * state.size, transcendentals=0
         ),
+        compiler_params=pltpu.CompilerParams(vmem_limit_bytes=FULL_GRANT),
         name="pack_strips",
     )(jnp.asarray(face_selector(columns), bf16), state)
 
 
-def pick_groups(me, groups, first, count, block):
+def pick_groups(me, groups, first, count):
     n, _, rows, columns = groups.shape
 
-    def kernel(me_ref, *refs):
-        for j in range(n - 1):
-            refs[n - 1 + j][...] = refs[j][0]
-
-    def chosen(j):
-        return lambda i, me: (lax.rem(me[0] + j, n), first // block + i, 0, 0)
+    def kernel(me_ref, groups_ref, *refs):
+        copies = []
+        for j in range(1, n):
+            part = groups_ref.at[me_ref[0] ^ j, pl.ds(first, count)]
+            copies.append(pltpu.make_async_copy(part, refs[j - 1], refs[-1].at[j - 1]))
+            copies[-1].start()
+        for copy in copies:
+            copy.wait()
 
     size = (n - 1) * count * rows * columns
     return pl.pallas_call(
         kernel,
-        grid_spec=pltpu.PrefetchScalarGridSpec(
-            num_scalar_prefetch=1,
-            grid=(count // block,),
-            in_specs=[pl.BlockSpec((1, block, rows, columns), chosen(j)) for j in range(1, n)],
-            out_specs=[pl.BlockSpec((block, rows, columns), lambda i, me: (i, 0, 0))] * (n - 1),
-        ),
+        in_specs=[
+            pl.BlockSpec(memory_space=pltpu.SMEM),
+            pl.BlockSpec(memory_space=pltpu.HBM),
+        ],
+        out_specs=[pl.BlockSpec(memory_space=pltpu.VMEM)] * (n - 1),
         out_shape=[jax.ShapeDtypeStruct((count, rows, columns), groups.dtype)] * (n - 1),
+        scratch_shapes=[pltpu.SemaphoreType.DMA((n - 1,))],
         cost_estimate=pl.CostEstimate(flops=0, bytes_accessed=4 * size, transcendentals=0),
+        compiler_params=pltpu.CompilerParams(vmem_limit_bytes=FULL_GRANT),
         name="pick_groups",
-    )(me, *[groups] * (n - 1))
-
-
-def local_part(state, mixed, speed_in, density, strips, source, flips):
+    )(me, groups)
+
+
+def local_part(state, rates, speed_in, density, strips, source, flips):
     owned, chans, rows, columns = state.shape
     patches = strips.shape[1]
     per = rows // patches
     wide = chans * per
     step = columns // per
-
-    def kernel(src_ref, flip_ref, turn_ref, place_ref, x_ref, m_ref, in_ref, den_ref, g0_ref, g1_ref, *refs):
-        o_ref = refs[-1]
+    inner, outer = bands(columns)
+
+    def kernel(
+        src_ref, flip_ref, turn_ref, inner_ref, outer_ref, rates_ref, x_ref, in_ref, den_ref, g0_ref, g1_ref,
+        o_ref, plain, mixed,
+    ):
         s, k = pl.program_id(0), pl.program_id(1)
 
         def turned(ref, face):
@@ -132,24 +159,26 @@
             return jnp.dot(stacked, turn, preferred_element_type=f32)
 
         low, high = turned(g0_ref, 0), turned(g1_ref, 1)
-        lane = lax.broadcasted_iota(jnp.int32, (step * per, columns), 1)
-        speed = jnp.broadcast_to(-section_step * in_ref[...], (step, per, columns)).reshape(-1, columns)
+        plain[...] = x_ref[0].reshape(wide, columns).astype(f32)
+        for r in range(0, per, 2):
+            pair = [plain[pl.ds(r + i, chans, stride=per), :] for i in range(2)]
+            both = jnp.concatenate(pair, 1).astype(bf16)
+            mix = jnp.dot(rates_ref[...], both, preferred_element_type=f32)
+            for i in range(2):
+                mixed[pl.ds(r + i, chans, stride=per), :] = mix[:, i * columns : (i + 1) * columns]
+        scale = -section_step / SCALE
+        speed = jnp.broadcast_to(scale * in_ref[...], (step, per, columns)).reshape(-1, columns)
         dens = jnp.broadcast_to(section_step * den_ref[...], (step, per, columns)).reshape(-1, columns)
         for i in range(chans // step):
-            both = jnp.concatenate([low[i * SUB : (i + 1) * SUB], high[i * SUB : (i + 1) * SUB]], 0)
-            ghost = lax.dot_general(
-                both.astype(bf16), place_ref[...], (((0,), (0,)), ((), ())), preferred_element_type=f32
+            ghost = jnp.concatenate([low[i * SUB : (i + 1) * SUB], high[i * SUB : (i + 1) * SUB]], 0)
+            cells = x_ref[0, i * step : (i + 1) * step].reshape(step * per, columns)
+            swept = jnp.dot(cells, inner_ref[...], preferred_element_type=f32) + lax.dot_general(
+                ghost.astype(bf16), outer_ref[...], (((0,), (0,)), ((), ())), preferred_element_type=f32
             )
-            x = x_ref[0, i * step : (i + 1) * step].reshape(step * per, columns).astype(f32)
-            smooth = (1.0 - filter_sigma * high_pass[5]) * x
-            slope = jnp.zeros_like(x)
-            for j in range(1, DEPTH + 1):
-                after = pltpu.roll(jnp.where(lane < j, ghost, x), columns - j, 1)
-                before = pltpu.roll(jnp.where(lane >= columns - j, ghost, x), j, 1)
-                smooth = smooth - (filter_sigma * high_pass[5 + j]) * (after + before)
-                slope = slope + deriv_coef[j - 1] * (after - before)
-            mix = m_ref[0, i * step : (i + 1) * step].reshape(step * per, columns)
-            base = smooth + speed * slope + dens * mix
+            high_part = swept[:, :columns]
+            slope = swept[:, columns : 2 * columns] + swept[:, 2 * columns :]
+            here = pl.ds(i * step * per, step * per)
+            base = plain[here, :] - high_part + speed * slope + dens * mixed[here, :]
             o_ref[0, i * step : (i + 1) * step] = base.reshape(step, per, columns)
 
     def cells(s, k, *_):
@@ -157,6 +186,9 @@
 
     def line(s, k, *_):
         return (s, k, 0)
+
+    def fixed(s, k, *_):
+        return (0, 0)
 
     def ghosts(face):
         return lambda s, k, src, flip: (src[(s * 2 + face) * patches + k], k, 0, 0)
@@ -168,8 +200,9 @@
             grid=(owned, patches),
             in_specs=[
                 pl.BlockSpec((2, columns, columns), lambda s, k, *_: (0, 0, 0)),
-                pl.BlockSpec((2 * SUB, columns), lambda s, k, *_: (0, 0)),
-                pl.BlockSpec((1, chans, per, columns), cells),
+                pl.BlockSpec(inner.shape, fixed),
+                pl.BlockSpec(outer.shape, fixed),
+                pl.BlockSpec(rates.shape, fixed),
                 pl.BlockSpec((1, chans, per, columns), cells),
                 pl.BlockSpec((1, per, columns), line),
                 pl.BlockSpec((1, per, columns), line),
@@ -177,19 +210,22 @@
                 pl.BlockSpec((1, 1, SUB, wide), ghosts(1)),
             ],
             out_specs=pl.BlockSpec((1, chans, per, columns), cells),
+            scratch_shapes=[pltpu.VMEM((wide, columns), f32), pltpu.VMEM((wide, columns), f32)],
         ),
         out_shape=jax.ShapeDtypeStruct(state.shape, f32),
         cost_estimate=pl.CostEstimate(
-            flops=60 * state.size, bytes_accessed=10 * state.size, transcendentals=0
-        ),
+            flops=1000 * state.size, bytes_accessed=8 * state.size, transcendentals=0
+        ),
+        compiler_params=pltpu.CompilerParams(vmem_limit_bytes=GRANT),
         name="local_part",
     )(
         source.reshape(-1),
         flips.reshape(-1),
         jnp.asarray(flip_pair(columns, per), bf16),
-        jnp.asarray(ghost_placer(columns), bf16),
+        jnp.asarray(inner, bf16),
+        jnp.asarray(outer, bf16),
+        rates,
         state,
-        mixed,
         speed_in,
         density,
         strips,
@@ -229,6 +265,7 @@
         cost_estimate=pl.CostEstimate(
             flops=2 * n * rows * size, bytes_accessed=4 * size, transcendentals=0
         ),
+        compiler_params=pltpu.CompilerParams(vmem_limit_bytes=GRANT),
         name="wall_product",
     )(me, operator, groups, *arrived)
 
@@ -242,7 +279,7 @@
     def kernel(me_ref, speed_ref, base_ref, *refs):
         o_ref = refs[-1]
         for j in range(n):
-            group = lax.rem(me_ref[0] + (n - j), n)
+            group = me_ref[0] ^ j
             speed = -section_step * speed_ref[group // per_slot]
             o_ref[group] = (base_ref[group] + speed[None] * refs[j][...].astype(f32)).astype(bf16)
 
@@ -261,15 +298,51 @@
         out_shape=jax.ShapeDtypeStruct(base.shape, bf16),
         input_output_aliases={} if fresh else {3 + n: 0},
         cost_estimate=pl.CostEstimate(flops=2 * size, bytes_accessed=8 * size, transcendentals=0),
+        compiler_params=pltpu.CompilerParams(vmem_limit_bytes=GRANT),
         name="finish",
     )(me, speed_wall, base, *normals, *([] if fresh else [out]))
 
 
+def finish_last(me, base, speed_wall, normals, out, first):
+    n, count, rows, columns = base.shape
+    per_slot = n // speed_wall.shape[0]
+
+    def kernel(me_ref, speed_ref, base_ref, *refs):
+        o_ref, done, sems = refs[n + 1], refs[n + 2], refs[n + 3]
+        copies = []
+        for j in range(n):
+            group = me_ref[0] ^ j
+            speed = -section_step * speed_ref[group // per_slot]
+            done[j] = (base_ref[group] + speed[None] * refs[j][...].astype(f32)).astype(bf16)
+            copies.append(
+                pltpu.make_async_copy(done.at[j], o_ref.at[group, pl.ds(first, count)], sems.at[j])
+            )
+            copies[-1].start()
+        for copy in copies:
+            copy.wait()
+
+    here = pl.BlockSpec(memory_space=pltpu.VMEM)
+    size = n * count * rows * columns
+    return pl.pallas_call(
+        kernel,
+        in_specs=[pl.BlockSpec(memory_space=pltpu.SMEM)]
+        + [here] * (n + 2)
+        + [pl.BlockSpec(memory_space=pl.ANY)],
+        out_specs=pl.BlockSpec(memory_space=pl.ANY),
+        out_shape=jax.ShapeDtypeStruct(out.shape, bf16),
+        scratch_shapes=[pltpu.VMEM((n, count, rows, columns), bf16), pltpu.SemaphoreType.DMA((n,))],
+        input_output_aliases={3 + n: 0},
+        cost_estimate=pl.CostEstimate(flops=2 * size, bytes_accessed=8 * size, transcendentals=0),
+        compiler_params=pltpu.CompilerParams(vmem_limit_bytes=GRANT),
+        name="finish_last",
+    )(me, speed_wall, base, *normals, out)
+
+
 def chunk_blocks(blocks):
-    if blocks < 4:
+    if blocks < 5:
         return [1] * blocks
-    middle = (blocks - 2) // 2
-    return [1, middle, blocks - 2 - middle, 1]
+    middle = (blocks - 3) // 2
+    return [1, middle, blocks - 3 - middle, 1, 1]
 
 
 def sizes(n, owned, chans):
@@ -285,7 +358,7 @@
     items, block = sizes(n, owned, chans)
     groups = state.reshape(n, items, rows, columns)
     where = me.astype(jnp.int32).reshape(1)
-    shifts = [[(i, (i + j) % n) for i in range(n)] for j in range(n)]
+    partners = [[(i, i ^ j) for i in range(n)] for j in range(n)]
 
     chunks, first = [], 0
     for size in chunk_blocks(items // block):
@@ -295,12 +368,12 @@
     def send(pieces):
         came = []
         for j in range(1, n):
-            came.append(lax.ppermute(pieces[j - 1], "line", shifts[j]))
+            came.append(lax.ppermute(pieces[j - 1], "line", partners[j]))
         return came
 
     arrived = []
     for first, count in chunks:
-        picked = pick_groups(where, groups, first, count, block)
+        picked = pick_groups(where, groups, first, count)
         arrived.append(send(picked))
 
     strips = pack_strips(state, patches)
@@ -312,24 +385,26 @@
     per_device = 2 * owned
     held = ((source // per_device) ^ mine) * per_device + source % per_device
 
-    tiles = wall_op.reshape(n, rows, n, rows)[:, :, ::-1]
-    tiles = jnp.concatenate([tiles, tiles], 0)
-    tiles = lax.dynamic_slice_in_dim(tiles, me, n, 0)
-    tiles = jnp.concatenate([tiles, tiles], 2)
-    operator = lax.dynamic_slice_in_dim(tiles, n - 1 - me, n, 2).reshape(n * rows, n * rows)
-
-    mixed = jnp.einsum("ce,belp->bclp", rates, state, preferred_element_type=f32)
-
-    base = local_part(state, mixed, speed_in, density, gathered, held.astype(jnp.int32), patch_flip)
+    place = jnp.arange(n * rows, dtype=jnp.int32)
+    moved = (((place // rows) ^ me) * rows + place % rows)[:, None] == place[None, :]
+    moved = moved.astype(bf16)
+    operator = jnp.dot(moved, wall_op, preferred_element_type=f32).astype(bf16)
+    operator = jnp.dot(operator, moved, preferred_element_type=f32).astype(bf16)
+
+    base = local_part(state, rates, speed_in, density, gathered, held.astype(jnp.int32), patch_flip)
     base = base.reshape(n, items, rows, columns)
+    tail = lax.slice_in_dim(base, chunks[-1][0], items, axis=1)
 
     returned = []
     for (first, count), came in zip(chunks, arrived):
         products = wall_product(where, groups, operator, came, first, block)
         returned.append([products[0]] + send(products[1:]))
     out = None
-    for (first, count), normals in zip(chunks, returned):
-        out = finish(where, base, speed_wall, normals, out, first, block)
+    for k, ((first, count), normals) in enumerate(zip(chunks, returned)):
+        if k < len(chunks) - 1:
+            out = finish(where, base, speed_wall, normals, out, first, block)
+        else:
+            out = finish_last(where, tail, speed_wall, normals, out, first)
     return out.reshape(state.shape)
 
 

time: 355 us -> 322 us (0.907)
  the two profiles are of different devices: /device:TPU:30 before, /device:TPU:16 now
where the time goes in v2:
time: 322 us
  waiting for transfers between devices  179 us (56%)
  starting transfers between devices  66.9 us (21%)
  Pallas kernels  47.9 us (15%)
  local copies, waits for them, and re-layouts  25.6 us (8%)
    ppermute x30, waiting for transfers between devices, send(): came.append(lax.ppermute(pieces[j - 1], 'line', partners[j]))  172 us
    ppermute x30, starting transfers between devices, send(): came.append(lax.ppermute(pieces[j - 1], 'line', partners[j]))  61.2 us
    unnamed x89, local copies, waits for them, and re-layouts  23.7 us
    pallas_call x1, Pallas kernels, local_part(): pl.pallas_call(kernel, grid_spec=pltpu.PrefetchScalarGridSpec(num_scalar_...  20.2 us
    pallas_call x5, Pallas kernels, pick_groups(): pl.pallas_call(kernel, in_specs=[pl.BlockSpec(memory_space=pltpu.SMEM), p...  10.6 us
    pallas_call x4, Pallas kernels, finish(): pl.pallas_call(kernel, grid_spec=pltpu.PrefetchScalarGridSpec(num_scalar_...  6.83 us
    ppermute x7, waiting for transfers between devices, body(): lax.ppermute(strips, 'blk', [(i, i ^ r) for i in range(nblk)])  6.5 us
  transfers between devices with their start and end apart: 37, of which 12 were waited for; matrix products, arithmetic and copies ran while one was open for 3% of the time, Pallas kernels for 14%

profile of v2, /device:TPU:16, one launch (start us, length us, event | category | flops | bytes accessed | tf_op | source)
XLA Modules:
  0.0 321.7 jit_solution(13114673027357857107)
XLA Ops:
  0.0 1.9 pick_groups.9
  1.9 1.6 collective-permute-start.31
  3.8 1.6 collective-permute-start.33
  5.4 2.5 pick_groups.8
  8.0 2.5 collective-permute-start.25
  10.5 1.8 pick_groups.6
  12.4 5.2 %pack_strips.1 = bf16[4,2,4,8,1408]{4,3,2,1,0:T(8,128)(2,1)} custom-call(bf16[16,128]{1,0:T(8,128)(2,1)} %constant.114.clone.pick_ref, bf16[4,88,64,128]{3,2,1,0:T(8,128)(2,1)} %own_ref.9), custom_call_target="tpu_custom_call" | custom-call | flops 92274688 | bytes 8650752 | tf_op jit(solution)/shard_map/pack_strips/pallas_call | solution.py:94
  17.6 2.0 constant_dynamic-update-slice_fusion.7
  19.6 2.6 pick_groups.7
  22.3 1.8 pick_groups.5
  25.4 2.9 collective-permute-start.15
  29.0 0.9 collective-permute-start.7
  30.6 0.8 collective-permute-start.8
  31.7 1.5 collective-permute-done.14.refs_1_
  33.9 3.5 %collective-permute-start.26 = (bf16[32,64,128]{2,1,0:T(8,128)(2,1)S(1)}, bf16[32,64,128]{2,1,0:T(8,128)(2,1)S(1)}, u32[]{:S(2)}, u32[]{:S(2)}) collective-permute-start(bf16[32,64,128]{2,1,0:T(8,128)(2,1)S(1)} %copy-done.35), channel_id=1, source_target_pairs={{0,2},{1,3},{2,0},{3,1},{4,6},{5,7},{6,4},{7,5},{8,10},{9,11},{10,... | collective-permute-start | bytes 1572872 | tf_op jit(solution)/shard_map/ppermute | solution.py:371
  37.5 20.5 %collective-permute-done.15.refs_2_ = bf16[8,64,128]{2,1,0:T(8,128)(2,1)S(1)} collective-permute-done((bf16[8,64,128]{2,1,0:T(8,128)(2,1)S(1)}, bf16[8,64,128]{2,1,0:T(8,128)(2,1)S(1)}, u32[]{:S(2)}, u32[]{:S(2)}) %collective-permute-start.15) | collective-permute-done | bytes 131104 | tf_op jit(solution)/shard_map/ppermute | solution.py:371
  58.6 0.8 collective-permute-start.27
  60.7 1.5 collective-permute-start.9
  62.3 31.7 %collective-permute-done.9.refs_2_ = bf16[8,64,128]{2,1,0:T(8,128)(2,1)S(1)} collective-permute-done((bf16[8,64,128]{2,1,0:T(8,128)(2,1)}, bf16[8,64,128]{2,1,0:T(8,128)(2,1)S(1)}, u32[]{:S(2)}, u32[]{:S(2)}) %collective-permute-start.9) | collective-permute-done | bytes 131104 | tf_op jit(solution)/shard_map/ppermute | solution.py:371
  95.5 1.6 collective-permute-start.1
  98.2 2.6 copy-done.1
  100.9 0.9 copy-done.9
  101.8 0.9 copy-done.11
  102.7 0.9 wall_product.9
  105.6 23.4 %collective-permute-done.20.refs_1_ = bf16[32,64,128]{2,1,0:T(8,128)(2,1)S(1)} collective-permute-done((bf16[32,64,128]{2,1,0:T(8,128)(2,1)}, bf16[32,64,128]{2,1,0:T(8,128)(2,1)S(1)}, u32[]{:S(2)}, u32[]{:S(2)}) %collective-permute-start.20) | collective-permute-done | bytes 524320 | tf_op jit(solution)/shard_map/ppermute | solution.py:371
  129.0 2.5 collective-permute-start.34
  131.5 0.8 fusion.4
  132.4 0.8 reshape.73.flip_ref
  133.1 2.6 copy-done.2
  135.8 0.9 copy-done.7
  136.7 0.9 copy-done.13
  137.6 0.9 copy-done.15
  139.9 1.3 wall_product.8
  141.2 1.7 collective-permute-start.3
  142.9 1.3 wall_product.7
  144.3 0.8 collective-permute-start.35
  145.1 0.8 collective-permute-start.36
  145.8 1.2 constant_dynamic-update-slice_fusion.6
  147.0 7.1 %collective-permute-done.35.refs_2_ = bf16[8,64,128]{2,1,0:T(8,128)(2,1)S(1)} collective-permute-done((bf16[8,64,128]{2,1,0:T(8,128)(2,1)S(1)}, bf16[8,64,128]{2,1,0:T(8,128)(2,1)S(1)}, u32[]{:S(2)}, u32[]{:S(2)}) %collective-permute-start.35) | collective-permute-done | bytes 131104 | tf_op jit(solution)/shard_map/ppermute | solution.py:371
  154.1 2.7 collective-permute-done.36.refs_3_
  156.8 1.4 collective-permute-start.5
  158.8 1.2 constant_dynamic-update-slice_fusion.5
  160.0 1.2 constant_dynamic-update-slice_fusion.4
  161.2 2.1 collective-permute-start.16
  163.4 12.9 %collective-permute-done.16.refs_1_ = bf16[8,64,128]{2,1,0:T(8,128)(2,1)S(1)} collective-permute-done((bf16[8,64,128]{2,1,0:T(8,128)(2,1)S(1)}, bf16[8,64,128]{2,1,0:T(8,128)(2,1)S(1)}, u32[]{:S(2)}, u32[]{:S(2)}) %collective-permute-start.16) | collective-permute-done | bytes 131104 | tf_op jit(solution)/shard_map/ppermute | solution.py:371
  176.3 20.7 %collective-permute-start.29 = (bf16[32,64,128]{2,1,0:T(8,128)(2,1)S(1)}, bf16[32,64,128]{2,1,0:T(8,128)(2,1)S(1)}, u32[]{:S(2)}, u32[]{:S(2)}) collective-permute-start(bf16[32,64,128]{2,1,0:T(8,128)(2,1)S(1)} %get-tuple-element.66), channel_id=1, source_target_pairs={{0,2},{1,3},{2,0},{3,1},{4,6},{5,7},{6,4},{7,5},{8,10},{9,11},{10,... | collective-permute-start | bytes 1572872 | tf_op jit(solution)/shard_map/ppermute | solution.py:371
  197.0 6.5 %collective-permute-done.4 = bf16[4,2,4,8,1408]{4,3,2,1,0:T(8,128)(2,1)S(1)} collective-permute-done((bf16[4,2,4,8,1408]{4,3,2,1,0:T(8,128)(2,1)S(1)}, bf16[4,2,4,8,1408]{4,3,2,1,0:T(8,128)(2,1)S(1)}, u32[]{:S(2)}, u32[]{:S(2)}) %collective-permute-start.4) | collective-permute-done | bytes 720928 | tf_op jit(solution)/shard_map/ppermute | solution.py:382
  203.4 2.0 collective-permute-start.30
  205.4 1.9 collective-permute-start.22
  207.4 1.6 collective-permute-start.24
  209.2 14.4 %collective-permute-done.29.refs_2_ = bf16[32,64,128]{2,1,0:T(8,128)(2,1)S(1)} collective-permute-done((bf16[32,64,128]{2,1,0:T(8,128)(2,1)S(1)}, bf16[32,64,128]{2,1,0:T(8,128)(2,1)S(1)}, u32[]{:S(2)}, u32[]{:S(2)}) %collective-permute-start.29) | collective-permute-done | bytes 524320 | tf_op jit(solution)/shard_map/ppermute | solution.py:371
  223.6 3.4 %collective-permute-start.17 = (bf16[8,64,128]{2,1,0:T(8,128)(2,1)S(1)}, bf16[8,64,128]{2,1,0:T(8,128)(2,1)S(1)}, u32[]{:S(2)}, u32[]{:S(2)}) collective-permute-start(bf16[8,64,128]{2,1,0:T(8,128)(2,1)S(1)} %get-tuple-element.52), channel_id=1, source_target_pairs={{0,2},{1,3},{2,0},{3,1},{4,6},{5,7},{6,4},{7,5},{8,10},{9,11},{10,... | collective-permute-start | bytes 393224 | tf_op jit(solution)/shard_map/ppermute | solution.py:371
  227.0 35.9 %collective-permute-done.30.refs_3_ = bf16[32,64,128]{2,1,0:T(8,128)(2,1)S(1)} collective-permute-done((bf16[32,64,128]{2,1,0:T(8,128)(2,1)S(1)}, bf16[32,64,128]{2,1,0:T(8,128)(2,1)S(1)}, u32[]{:S(2)}, u32[]{:S(2)}) %collective-permute-start.30) | collective-permute-done | bytes 524320 | tf_op jit(solution)/shard_map/ppermute | solution.py:371
  263.0 2.5 collective-permute-start.18
  265.5 11.6 %collective-permute-done.23.refs_2_ = bf16[32,64,128]{2,1,0:T(8,128)(2,1)S(1)} collective-permute-done((bf16[32,64,128]{2,1,0:T(8,128)(2,1)S(1)}, bf16[32,64,128]{2,1,0:T(8,128)(2,1)S(1)}, u32[]{:S(2)}, u32[]{:S(2)}) %collective-permute-start.23) | collective-permute-done | bytes 524320 | tf_op jit(solution)/shard_map/ppermute | solution.py:371
  277.1 3.4 %collective-permute-start.11 = (bf16[8,64,128]{2,1,0:T(8,128)(2,1)S(1)}, bf16[8,64,128]{2,1,0:T(8,128)(2,1)S(1)}, u32[]{:S(2)}, u32[]{:S(2)}) collective-permute-start(bf16[8,64,128]{2,1,0:T(8,128)(2,1)S(1)} %get-tuple-element.45), channel_id=1, source_target_pairs={{0,2},{1,3},{2,0},{3,1},{4,6},{5,7},{6,4},{7,5},{8,10},{9,11},{10,... | collective-permute-start | bytes 393224 | tf_op jit(solution)/shard_map/ppermute | solution.py:371
  280.4 10.7 %collective-permute-done.24.refs_3_ = bf16[32,64,128]{2,1,0:T(8,128)(2,1)S(1)} collective-permute-done((bf16[32,64,128]{2,1,0:T(8,128)(2,1)S(1)}, bf16[32,64,128]{2,1,0:T(8,128)(2,1)S(1)}, u32[]{:S(2)}, u32[]{:S(2)}) %collective-permute-start.24) | collective-permute-done | bytes 524320 | tf_op jit(solution)/shard_map/ppermute | solution.py:371
  291.1 2.5 collective-permute-start.12
  293.6 20.2 %local_part.1.base_ref = f32[4,88,64,128]{3,2,1,0:T(8,128)S(1)} custom-call(s32[32]{0:T(128)S(1)} %reshape.72.src_ref, s32[32]{0:T(128)S(1)} %reshape.73.flip_ref, bf16[2,128,128]{2,1,0:T(8,128)(2,1)S(1)} %copy-done.25, bf16[128,384]{1,0:T(8,128)(2,1)S(1)} %copy-done.24, bf16[16,384]{1,0:T(8,128)(2,1)S(1)} %copy-done.27, bf16[88,88]{1,0:T(8,128)(2,1)S(1)} %copy-done.26, ...), custom_call_target="tpu_custom_call" | custom-call | flops 2883584000 | bytes 23068672 | tf_op jit(solution)/shard_map/local_part/pallas_call | solution.py:196
  314.0 1.0 finish.4.refs_4_
  315.1 2.4 finish.5.refs_4_
  317.4 2.4 finish.6.refs_4_
  319.8 1.0 finish.7.refs_4_
  320.9 0.9 finish_last.1
  (132 shorter events, 13.2 us)
Async XLA Ops:
  0.0 31.4 %copy-start = (bf16[256,256]{1,0:T(8,128)(2,1)S(1)}, bf16[256,256]{1,0:T(8,128)(2,1)}, u32[]{:S(2)}) copy-start(bf16[256,256]{1,0:T(8,128)(2,1)} %param.19) | copy-start | bytes 393220
  1.9 22.3 %collective-permute-start.31 = (bf16[8,64,128]{2,1,0:T(8,128)(2,1)}, bf16[8,64,128]{2,1,0:T(8,128)(2,1)S(1)}, u32[]{:S(2)}, u32[]{:S(2)}) collective-permute-start(bf16[8,64,128]{2,1,0:T(8,128)(2,1)} %get-tuple-element.68), channel_id=1, source_target_pairs={{0,1},{1,0},{2,3},{3,2},{4,5},{5,4},{6,7},{7,6},{8,9},{9,8},{10,11... | collective-permute-start | bytes 393224 | tf_op jit(solution)/shard_map/ppermute | solution.py:371
  3.5 21.2 %collective-permute-start.32 = (bf16[8,64,128]{2,1,0:T(8,128)(2,1)}, bf16[8,64,128]{2,1,0:T(8,128)(2,1)S(1)}, u32[]{:S(2)}, u32[]{:S(2)}) collective-permute-start(bf16[8,64,128]{2,1,0:T(8,128)(2,1)} %get-tuple-element.69), channel_id=1, source_target_pairs={{0,2},{1,3},{2,0},{3,1},{4,6},{5,7},{6,4},{7,5},{8,10},{9,11},{10,... | collective-permute-start | bytes 393224 | tf_op jit(solution)/shard_map/ppermute | solution.py:371
  3.8 24.5 %collective-permute-start.33 = (bf16[8,64,128]{2,1,0:T(8,128)(2,1)}, bf16[8,64,128]{2,1,0:T(8,128)(2,1)S(1)}, u32[]{:S(2)}, u32[]{:S(2)}) collective-permute-start(bf16[8,64,128]{2,1,0:T(8,128)(2,1)} %get-tuple-element.70), channel_id=1, source_target_pairs={{0,3},{1,2},{2,1},{3,0},{4,7},{5,6},{6,5},{7,4},{8,11},{9,10},{10,... | collective-permute-start | bytes 393224 | tf_op jit(solution)/shard_map/ppermute | solution.py:371
  8.0 86.7 %collective-permute-start.25 = (bf16[32,64,128]{2,1,0:T(8,128)(2,1)}, bf16[32,64,128]{2,1,0:T(8,128)(2,1)S(1)}, u32[]{:S(2)}, u32[]{:S(2)}) collective-permute-start(bf16[32,64,128]{2,1,0:T(8,128)(2,1)} %get-tuple-element.61), channel_id=1, source_target_pairs={{0,1},{1,0},{2,3},{3,2},{4,5},{5,4},{6,7},{7,6},{8,9},{9,8},{10,11... | collective-permute-start | bytes 1572872 | tf_op jit(solution)/shard_map/ppermute | solution.py:371
  12.3 17.6 %collective-permute-start.13 = (bf16[8,64,128]{2,1,0:T(8,128)(2,1)}, bf16[8,64,128]{2,1,0:T(8,128)(2,1)S(1)}, u32[]{:S(2)}, u32[]{:S(2)}) collective-permute-start(bf16[8,64,128]{2,1,0:T(8,128)(2,1)} %get-tuple-element.47), channel_id=1, source_target_pairs={{0,1},{1,0},{2,3},{3,2},{4,5},{5,4},{6,7},{7,6},{8,9},{9,8},{10,11... | collective-permute-start | bytes 393224 | tf_op jit(solution)/shard_map/ppermute | solution.py:371
  19.6 4.5 %copy-start.37 = (bf16[8,64,128]{2,1,0:T(8,128)(2,1)S(1)}, bf16[8,64,128]{2,1,0:T(8,128)(2,1)}, u32[]{:S(2)}) copy-start(bf16[8,64,128]{2,1,0:T(8,128)(2,1)} %get-tuple-element.48) | copy-start | bytes 393220
  19.6 5.8 %copy-start.36 = (bf16[8,64,128]{2,1,0:T(8,128)(2,1)S(1)}, bf16[8,64,128]{2,1,0:T(8,128)(2,1)}, u32[]{:S(2)}) copy-start(bf16[8,64,128]{2,1,0:T(8,128)(2,1)} %get-tuple-element.49) | copy-start | bytes 393220
  19.6 14.3 %copy-start.35 = (bf16[32,64,128]{2,1,0:T(8,128)(2,1)S(1)}, bf16[32,64,128]{2,1,0:T(8,128)(2,1)}, u32[]{:S(2)}) copy-start(bf16[32,64,128]{2,1,0:T(8,128)(2,1)} %get-tuple-element.62) | copy-start | bytes 1572868
  19.6 42.6 %copy-start.33 = (s32[4,2,4]{2,1,0:T(2,128)S(1)}, s32[4,2,4]{2,1,0:T(2,128)}, u32[]{:S(2)}) copy-start(s32[4,2,4]{2,1,0:T(2,128)} %param.21) | copy-start | bytes 388
  19.6 75.8 %copy-start.38 = (s32[32]{0:T(128)S(1)}, s32[32]{0:T(128)}, u32[]{:S(2)}) copy-start(s32[32]{0:T(128)} %param.20) | copy-start | bytes 388
  24.1 9.1 %collective-permute-start.14 = (bf16[8,64,128]{2,1,0:T(8,128)(2,1)S(1)}, bf16[8,64,128]{2,1,0:T(8,128)(2,1)S(1)}, u32[]{:S(2)}, u32[]{:S(2)}) collective-permute-start(bf16[8,64,128]{2,1,0:T(8,128)(2,1)S(1)} %copy-done.37), channel_id=1, source_target_pairs={{0,2},{1,3},{2,0},{3,1},{4,6},{5,7},{6,4},{7,5},{8,10},{9,11},{10,... | collective-permute-start | bytes 393224 | tf_op jit(solution)/shard_map/ppermute | solution.py:371
  25.4 32.6 %collective-permute-start.15 = (bf16[8,64,128]{2,1,0:T(8,128)(2,1)S(1)}, bf16[8,64,128]{2,1,0:T(8,128)(2,1)S(1)}, u32[]{:S(2)}, u32[]{:S(2)}) collective-permute-start(bf16[8,64,128]{2,1,0:T(8,128)(2,1)S(1)} %copy-done.36), channel_id=1, source_target_pairs={{0,3},{1,2},{2,1},{3,0},{4,7},{5,6},{6,5},{7,4},{8,11},{9,10},{10,... | collective-permute-start | bytes 393224 | tf_op jit(solution)/shard_map/ppermute | solution.py:371
  29.0 30.4 %collective-permute-start.7 = (bf16[8,64,128]{2,1,0:T(8,128)(2,1)}, bf16[8,64,128]{2,1,0:T(8,128)(2,1)S(1)}, u32[]{:S(2)}, u32[]{:S(2)}) collective-permute-start(bf16[8,64,128]{2,1,0:T(8,128)(2,1)} %get-tuple-element.40), channel_id=1, source_target_pairs={{0,1},{1,0},{2,3},{3,2},{4,5},{5,4},{6,7},{7,6},{8,9},{9,8},{10,11... | collective-permute-start | bytes 393224 | tf_op jit(solution)/shard_map/ppermute | solution.py:371
  30.6 29.5 %collective-permute-start.8 = (bf16[8,64,128]{2,1,0:T(8,128)(2,1)}, bf16[8,64,128]{2,1,0:T(8,128)(2,1)S(1)}, u32[]{:S(2)}, u32[]{:S(2)}) collective-permute-start(bf16[8,64,128]{2,1,0:T(8,128)(2,1)} %get-tuple-element.41), channel_id=1, source_target_pairs={{0,2},{1,3},{2,0},{3,1},{4,6},{5,7},{6,4},{7,5},{8,10},{9,11},{10,... | collective-permute-start | bytes 393224 | tf_op jit(solution)/shard_map/ppermute | solution.py:371
  33.9 61.5 %collective-permute-start.26 = (bf16[32,64,128]{2,1,0:T(8,128)(2,1)S(1)}, bf16[32,64,128]{2,1,0:T(8,128)(2,1)S(1)}, u32[]{:S(2)}, u32[]{:S(2)}) collective-permute-start(bf16[32,64,128]{2,1,0:T(8,128)(2,1)S(1)} %copy-done.35), channel_id=1, source_target_pairs={{0,2},{1,3},{2,0},{3,1},{4,6},{5,7},{6,4},{7,5},{8,10},{9,11},{10,... | collective-permute-start | bytes 1572872 | tf_op jit(solution)/shard_map/ppermute | solution.py:371
  58.6 36.9 %collective-permute-start.27 = (bf16[32,64,128]{2,1,0:T(8,128)(2,1)}, bf16[32,64,128]{2,1,0:T(8,128)(2,1)S(1)}, u32[]{:S(2)}, u32[]{:S(2)}) collective-permute-start(bf16[32,64,128]{2,1,0:T(8,128)(2,1)} %get-tuple-element.63), channel_id=1, source_target_pairs={{0,3},{1,2},{2,1},{3,0},{4,7},{5,6},{6,5},{7,4},{8,11},{9,10},{10,... | collective-permute-start | bytes 1572872 | tf_op jit(solution)/shard_map/ppermute | solution.py:371
  60.1 37.1 %collective-permute-start.19 = (bf16[32,64,128]{2,1,0:T(8,128)(2,1)}, bf16[32,64,128]{2,1,0:T(8,128)(2,1)S(1)}, u32[]{:S(2)}, u32[]{:S(2)}) collective-permute-start(bf16[32,64,128]{2,1,0:T(8,128)(2,1)} %get-tuple-element.54), channel_id=1, source_target_pairs={{0,1},{1,0},{2,3},{3,2},{4,5},{5,4},{6,7},{7,6},{8,9},{9,8},{10,11... | collective-permute-start | bytes 1572872 | tf_op jit(solution)/shard_map/ppermute | solution.py:371
  60.7 33.3 %collective-permute-start.9 = (bf16[8,64,128]{2,1,0:T(8,128)(2,1)}, bf16[8,64,128]{2,1,0:T(8,128)(2,1)S(1)}, u32[]{:S(2)}, u32[]{:S(2)}) collective-permute-start(bf16[8,64,128]{2,1,0:T(8,128)(2,1)} %get-tuple-element.42), channel_id=1, source_target_pairs={{0,3},{1,2},{2,1},{3,0},{4,7},{5,6},{6,5},{7,4},{8,11},{9,10},{10,... | collective-permute-start | bytes 393224 | tf_op jit(solution)/shard_map/ppermute | solution.py:371
  94.6 34.4 %collective-permute-start.20 = (bf16[32,64,128]{2,1,0:T(8,128)(2,1)}, bf16[32,64,128]{2,1,0:T(8,128)(2,1)S(1)}, u32[]{:S(2)}, u32[]{:S(2)}) collective-permute-start(bf16[32,64,128]{2,1,0:T(8,128)(2,1)} %get-tuple-element.55), channel_id=1, source_target_pairs={{0,2},{1,3},{2,0},{3,1},{4,6},{5,7},{6,4},{7,5},{8,10},{9,11},{10,... | collective-permute-start | bytes 1572872 | tf_op jit(solution)/shard_map/ppermute | solution.py:371
  94.7 50.4 %collective-permute-start = (bf16[4,2,4,8,1408]{4,3,2,1,0:T(8,128)(2,1)}, bf16[4,2,4,8,1408]{4,3,2,1,0:T(8,128)(2,1)}, u32[]{:S(2)}, u32[]{:S(2)}) collective-permute-start(bf16[4,2,4,8,1408]{4,3,2,1,0:T(8,128)(2,1)} %pack_strips.1), channel_id=1, source_target_pairs={{0,4},{4,0},{8,12},{12,8},{16,20},{20,16},{24,28},{28,24},{1,5},{5... | collective-permute-start | bytes 2162696 | tf_op jit(solution)/shard_map/ppermute | solution.py:382
  95.4 45.8 %collective-permute-start.21 = (bf16[32,64,128]{2,1,0:T(8,128)(2,1)}, bf16[32,64,128]{2,1,0:T(8,128)(2,1)S(1)}, u32[]{:S(2)}, u32[]{:S(2)}) collective-permute-start(bf16[32,64,128]{2,1,0:T(8,128)(2,1)} %get-tuple-element.56), channel_id=1, source_target_pairs={{0,3},{1,2},{2,1},{3,0},{4,7},{5,6},{6,5},{7,4},{8,11},{9,10},{10,... | collective-permute-start | bytes 1572872 | tf_op jit(solution)/shard_map/ppermute | solution.py:371
  95.5 62.7 %collective-permute-start.1 = (bf16[4,2,4,8,1408]{4,3,2,1,0:T(8,128)(2,1)}, bf16[4,2,4,8,1408]{4,3,2,1,0:T(8,128)(2,1)}, u32[]{:S(2)}, u32[]{:S(2)}) collective-permute-start(bf16[4,2,4,8,1408]{4,3,2,1,0:T(8,128)(2,1)} %pack_strips.1), channel_id=1, source_target_pairs={{0,8},{4,12},{8,0},{12,4},{16,24},{20,28},{24,16},{28,20},{1,9},{5... | collective-permute-start | bytes 2162696 | tf_op jit(solution)/shard_map/ppermute | solution.py:382
  97.1 61.7 %collective-permute-start.2 = (bf16[4,2,4,8,1408]{4,3,2,1,0:T(8,128)(2,1)}, bf16[4,2,4,8,1408]{4,3,2,1,0:T(8,128)(2,1)}, u32[]{:S(2)}, u32[]{:S(2)}) collective-permute-start(bf16[4,2,4,8,1408]{4,3,2,1,0:T(8,128)(2,1)} %pack_strips.1), channel_id=1, source_target_pairs={{0,12},{4,8},{8,4},{12,0},{16,28},{20,24},{24,20},{28,16},{1,13},{... | collective-permute-start | bytes 2162696 | tf_op jit(solution)/shard_map/ppermute | solution.py:382
  98.2 2.6 copy-start.1
  101.8 0.9 copy-start.11
  102.7 28.8 %copy-start.34 = (s32[4,2]{1,0:T(4,128)S(1)}, s32[4,2]{1,0:T(4,128)}, u32[]{:S(2)}) copy-start(s32[4,2]{1,0:T(4,128)} %iota_add_fusion) | copy-start | bytes 100
  129.0 15.3 %collective-permute-start.34 = (bf16[8,64,128]{2,1,0:T(8,128)(2,1)}, bf16[8,64,128]{2,1,0:T(8,128)(2,1)S(1)}, u32[]{:S(2)}, u32[]{:S(2)}) collective-permute-start(bf16[8,64,128]{2,1,0:T(8,128)(2,1)} %get-tuple-element.72), channel_id=1, source_target_pairs={{0,1},{1,0},{2,3},{3,2},{4,5},{5,4},{6,7},{7,6},{8,9},{9,8},{10,11... | collective-permute-start | bytes 393224 | tf_op jit(solution)/shard_map/ppermute | solution.py:371
  133.1 2.6 copy-start.2
  137.6 0.9 copy-start.15
  138.5 0.9 copy-start.17
  138.5 1.0 copy-start.19
  138.5 1.0 copy-start.21
  139.5 1.7 copy-start.32
  139.5 6.3 %slice-start = ((s8[5767168]{0:T(1024)(128)(4,1)}), s8[4194304]{0:T(1024)(128)(4,1)S(1)}, s32[]{:S(2)}) async-start(s8[5767168]{0:T(1024)(128)(4,1)} %bitcast.3), calls=%async_computation | async-start | bytes 8388608
  139.8 4.5 %copy-start.31 = (bf16[8,64,128]{2,1,0:T(8,128)(2,1)S(1)}, bf16[8,64,128]{2,1,0:T(8,128)(2,1)}, u32[]{:S(2)}) copy-start(bf16[8,64,128]{2,1,0:T(8,128)(2,1)} %copy-done.30) | copy-start | bytes 393220
  139.8 5.2 %copy-start.29 = (bf16[8,64,128]{2,1,0:T(8,128)(2,1)S(1)}, bf16[8,64,128]{2,1,0:T(8,128)(2,1)}, u32[]{:S(2)}) copy-start(bf16[8,64,128]{2,1,0:T(8,128)(2,1)} %copy-done.28) | copy-start | bytes 393220
  139.9 6.0 %slice-start.1 = ((s8[5767168]{0:T(1024)(128)(4,1)}), s8[1572864]{0:T(1024)(128)(4,1)S(1)}, s32[]{:S(2)}) async-start(s8[5767168]{0:T(1024)(128)(4,1)} %bitcast.3), calls=%async_computation.1 | async-start | bytes 3145728
  141.2 20.0 %collective-permute-start.3 = (bf16[4,2,4,8,1408]{4,3,2,1,0:T(8,128)(2,1)S(1)}, bf16[4,2,4,8,1408]{4,3,2,1,0:T(8,128)(2,1)S(1)}, u32[]{:S(2)}, u32[]{:S(2)}) collective-permute-start(bf16[4,2,4,8,1408]{4,3,2,1,0:T(8,128)(2,1)S(1)} %copy-done.32), channel_id=1, source_target_pairs={{0,16},{4,20},{8,24},{12,28},{16,0},{20,4},{24,8},{28,12},{1,17},{... | collective-permute-start | bytes 2162696 | tf_op jit(solution)/shard_map/ppermute | solution.py:382
  144.2 149.4 %copy-start.4 = (f32[4,64,128]{2,1,0:T(8,128)S(1)}, f32[4,64,128]{2,1,0:T(8,128)}, u32[]{:S(2)}) copy-start(f32[4,64,128]{2,1,0:T(8,128)} %in_ref.1) | copy-start | bytes 393220
  144.2 149.4 %copy-start.5 = (f32[4,64,128]{2,1,0:T(8,128)S(1)}, f32[4,64,128]{2,1,0:T(8,128)}, u32[]{:S(2)}) copy-start(f32[4,64,128]{2,1,0:T(8,128)} %den_ref.1) | copy-start | bytes 393220
  144.2 149.4 %copy-start.24 = (bf16[128,384]{1,0:T(8,128)(2,1)S(1)}, bf16[128,384]{1,0:T(8,128)(2,1)}, u32[]{:S(2)}) copy-start(bf16[128,384]{1,0:T(8,128)(2,1)} %constant.116.clone.inner_ref) | copy-start | bytes 294916
  144.2 149.4 %copy-start.25 = (bf16[2,128,128]{2,1,0:T(8,128)(2,1)S(1)}, bf16[2,128,128]{2,1,0:T(8,128)(2,1)}, u32[]{:S(2)}) copy-start(bf16[2,128,128]{2,1,0:T(8,128)(2,1)} %constant.115.clone.turn_ref) | copy-start | bytes 196612
  144.3 149.3 %copy-start.26 = (bf16[88,88]{1,0:T(8,128)(2,1)S(1)}, bf16[88,88]{1,0:T(8,128)(2,1)}, u32[]{:S(2)}) copy-start(bf16[88,88]{1,0:T(8,128)(2,1)} %rates_ref.1) | copy-start | bytes 46468
  144.3 149.3 %copy-start.27 = (bf16[16,384]{1,0:T(8,128)(2,1)S(1)}, bf16[16,384]{1,0:T(8,128)(2,1)}, u32[]{:S(2)}) copy-start(bf16[16,384]{1,0:T(8,128)(2,1)} %constant.117.clone.outer_ref) | copy-start | bytes 36868
  144.3 9.8 %collective-permute-start.35 = (bf16[8,64,128]{2,1,0:T(8,128)(2,1)S(1)}, bf16[8,64,128]{2,1,0:T(8,128)(2,1)S(1)}, u32[]{:S(2)}, u32[]{:S(2)}) collective-permute-start(bf16[8,64,128]{2,1,0:T(8,128)(2,1)S(1)} %copy-done.31), channel_id=1, source_target_pairs={{0,2},{1,3},{2,0},{3,1},{4,6},{5,7},{6,4},{7,5},{8,10},{9,11},{10,... | collective-permute-start | bytes 393224 | tf_op jit(solution)/shard_map/ppermute | solution.py:371
  145.1 11.7 %collective-permute-start.36 = (bf16[8,64,128]{2,1,0:T(8,128)(2,1)S(1)}, bf16[8,64,128]{2,1,0:T(8,128)(2,1)S(1)}, u32[]{:S(2)}, u32[]{:S(2)}) collective-permute-start(bf16[8,64,128]{2,1,0:T(8,128)(2,1)S(1)} %copy-done.29), channel_id=1, source_target_pairs={{0,3},{1,2},{2,1},{3,0},{4,7},{5,6},{6,5},{7,4},{8,11},{9,10},{10,... | collective-permute-start | bytes 393224 | tf_op jit(solution)/shard_map/ppermute | solution.py:371
  154.1 49.3 %collective-permute-start.4 = (bf16[4,2,4,8,1408]{4,3,2,1,0:T(8,128)(2,1)S(1)}, bf16[4,2,4,8,1408]{4,3,2,1,0:T(8,128)(2,1)S(1)}, u32[]{:S(2)}, u32[]{:S(2)}) collective-permute-start(bf16[4,2,4,8,1408]{4,3,2,1,0:T(8,128)(2,1)S(1)} %copy-done.32), channel_id=1, source_target_pairs={{0,20},{4,16},{8,28},{12,24},{16,4},{20,0},{24,12},{28,8},{1,21},{... | collective-permute-start | bytes 2162696 | tf_op jit(solution)/shard_map/ppermute | solution.py:382
  156.8 48.6 %collective-permute-start.5 = (bf16[4,2,4,8,1408]{4,3,2,1,0:T(8,128)(2,1)S(1)}, bf16[4,2,4,8,1408]{4,3,2,1,0:T(8,128)(2,1)S(1)}, u32[]{:S(2)}, u32[]{:S(2)}) collective-permute-start(bf16[4,2,4,8,1408]{4,3,2,1,0:T(8,128)(2,1)S(1)} %copy-done.32), channel_id=1, source_target_pairs={{0,24},{4,28},{8,16},{12,20},{16,8},{20,12},{24,0},{28,4},{1,25},{... | collective-permute-start | bytes 2162696 | tf_op jit(solution)/shard_map/ppermute | solution.py:382
  158.2 49.1 %collective-permute-start.6 = (bf16[4,2,4,8,1408]{4,3,2,1,0:T(8,128)(2,1)S(1)}, bf16[4,2,4,8,1408]{4,3,2,1,0:T(8,128)(2,1)S(1)}, u32[]{:S(2)}, u32[]{:S(2)}) collective-permute-start(bf16[4,2,4,8,1408]{4,3,2,1,0:T(8,128)(2,1)S(1)} %copy-done.32), channel_id=1, source_target_pairs={{0,28},{4,24},{8,20},{12,16},{16,12},{20,8},{24,4},{28,0},{1,29},{... | collective-permute-start | bytes 2162696 | tf_op jit(solution)/shard_map/ppermute | solution.py:382
  158.8 48.6 %collective-permute-start.28 = (bf16[32,64,128]{2,1,0:T(8,128)(2,1)S(1)}, bf16[32,64,128]{2,1,0:T(8,128)(2,1)S(1)}, u32[]{:S(2)}, u32[]{:S(2)}) collective-permute-start(bf16[32,64,128]{2,1,0:T(8,128)(2,1)S(1)} %get-tuple-element.65), channel_id=1, source_target_pairs={{0,1},{1,0},{2,3},{3,2},{4,5},{5,4},{6,7},{7,6},{8,9},{9,8},{10,11... | collective-permute-start | bytes 1572872 | tf_op jit(solution)/shard_map/ppermute | solution.py:371
  161.2 15.1 %collective-permute-start.16 = (bf16[8,64,128]{2,1,0:T(8,128)(2,1)S(1)}, bf16[8,64,128]{2,1,0:T(8,128)(2,1)S(1)}, u32[]{:S(2)}, u32[]{:S(2)}) collective-permute-start(bf16[8,64,128]{2,1,0:T(8,128)(2,1)S(1)} %get-tuple-element.51), channel_id=1, source_target_pairs={{0,1},{1,0},{2,3},{3,2},{4,5},{5,4},{6,7},{7,6},{8,9},{9,8},{10,11... | collective-permute-start | bytes 393224 | tf_op jit(solution)/shard_map/ppermute | solution.py:371
  176.3 47.4 %collective-permute-start.29 = (bf16[32,64,128]{2,1,0:T(8,128)(2,1)S(1)}, bf16[32,64,128]{2,1,0:T(8,128)(2,1)S(1)}, u32[]{:S(2)}, u32[]{:S(2)}) collective-permute-start(bf16[32,64,128]{2,1,0:T(8,128)(2,1)S(1)} %get-tuple-element.66), channel_id=1, source_target_pairs={{0,2},{1,3},{2,0},{3,1},{4,6},{5,7},{6,4},{7,5},{8,10},{9,11},{10,... | collective-permute-start | bytes 1572872 | tf_op jit(solution)/shard_map/ppermute | solution.py:371
  203.4 59.5 %collective-permute-start.30 = (bf16[32,64,128]{2,1,0:T(8,128)(2,1)S(1)}, bf16[32,64,128]{2,1,0:T(8,128)(2,1)S(1)}, u32[]{:S(2)}, u32[]{:S(2)}) collective-permute-start(bf16[32,64,128]{2,1,0:T(8,128)(2,1)S(1)} %get-tuple-element.67), channel_id=1, source_target_pairs={{0,3},{1,2},{2,1},{3,0},{4,7},{5,6},{6,5},{7,4},{8,11},{9,10},{10,... | collective-permute-start | bytes 1572872 | tf_op jit(solution)/shard_map/ppermute | solution.py:371
  205.4 60.0 %collective-permute-start.22 = (bf16[32,64,128]{2,1,0:T(8,128)(2,1)S(1)}, bf16[32,64,128]{2,1,0:T(8,128)(2,1)S(1)}, u32[]{:S(2)}, u32[]{:S(2)}) collective-permute-start(bf16[32,64,128]{2,1,0:T(8,128)(2,1)S(1)} %get-tuple-element.58), channel_id=1, source_target_pairs={{0,1},{1,0},{2,3},{3,2},{4,5},{5,4},{6,7},{7,6},{8,9},{9,8},{10,11... | collective-permute-start | bytes 1572872 | tf_op jit(solution)/shard_map/ppermute | solution.py:371
  207.3 69.7 %collective-permute-start.23 = (bf16[32,64,128]{2,1,0:T(8,128)(2,1)S(1)}, bf16[32,64,128]{2,1,0:T(8,128)(2,1)S(1)}, u32[]{:S(2)}, u32[]{:S(2)}) collective-permute-start(bf16[32,64,128]{2,1,0:T(8,128)(2,1)S(1)} %get-tuple-element.59), channel_id=1, source_target_pairs={{0,2},{1,3},{2,0},{3,1},{4,6},{5,7},{6,4},{7,5},{8,10},{9,11},{10,... | collective-permute-start | bytes 1572872 | tf_op jit(solution)/shard_map/ppermute | solution.py:371
  207.4 83.7 %collective-permute-start.24 = (bf16[32,64,128]{2,1,0:T(8,128)(2,1)S(1)}, bf16[32,64,128]{2,1,0:T(8,128)(2,1)S(1)}, u32[]{:S(2)}, u32[]{:S(2)}) collective-permute-start(bf16[32,64,128]{2,1,0:T(8,128)(2,1)S(1)} %get-tuple-element.60), channel_id=1, source_target_pairs={{0,3},{1,2},{2,1},{3,0},{4,7},{5,6},{6,5},{7,4},{8,11},{9,10},{10,... | collective-permute-start | bytes 1572872 | tf_op jit(solution)/shard_map/ppermute | solution.py:371
  223.6 96.2 %collective-permute-start.17 = (bf16[8,64,128]{2,1,0:T(8,128)(2,1)S(1)}, bf16[8,64,128]{2,1,0:T(8,128)(2,1)S(1)}, u32[]{:S(2)}, u32[]{:S(2)}) collective-permute-start(bf16[8,64,128]{2,1,0:T(8,128)(2,1)S(1)} %get-tuple-element.52), channel_id=1, source_target_pairs={{0,2},{1,3},{2,0},{3,1},{4,6},{5,7},{6,4},{7,5},{8,10},{9,11},{10,... | collective-permute-start | bytes 393224 | tf_op jit(solution)/shard_map/ppermute | solution.py:371
  263.0 56.8 %collective-permute-start.18 = (bf16[8,64,128]{2,1,0:T(8,128)(2,1)S(1)}, bf16[8,64,128]{2,1,0:T(8,128)(2,1)S(1)}, u32[]{:S(2)}, u32[]{:S(2)}) collective-permute-start(bf16[8,64,128]{2,1,0:T(8,128)(2,1)S(1)} %get-tuple-element.53), channel_id=1, source_target_pairs={{0,3},{1,2},{2,1},{3,0},{4,7},{5,6},{6,5},{7,4},{8,11},{9,10},{10,... | collective-permute-start | bytes 393224 | tf_op jit(solution)/shard_map/ppermute | solution.py:371
  265.5 55.4 %collective-permute-start.10 = (bf16[8,64,128]{2,1,0:T(8,128)(2,1)S(1)}, bf16[8,64,128]{2,1,0:T(8,128)(2,1)S(1)}, u32[]{:S(2)}, u32[]{:S(2)}) collective-permute-start(bf16[8,64,128]{2,1,0:T(8,128)(2,1)S(1)} %get-tuple-element.44), channel_id=1, source_target_pairs={{0,1},{1,0},{2,3},{3,2},{4,5},{5,4},{6,7},{7,6},{8,9},{9,8},{10,11... | collective-permute-start | bytes 393224 | tf_op jit(solution)/shard_map/ppermute | solution.py:371
  277.1 43.8 %collective-permute-start.11 = (bf16[8,64,128]{2,1,0:T(8,128)(2,1)S(1)}, bf16[8,64,128]{2,1,0:T(8,128)(2,1)S(1)}, u32[]{:S(2)}, u32[]{:S(2)}) collective-permute-start(bf16[8,64,128]{2,1,0:T(8,128)(2,1)S(1)} %get-tuple-element.45), channel_id=1, source_target_pairs={{0,2},{1,3},{2,0},{3,1},{4,6},{5,7},{6,4},{7,5},{8,10},{9,11},{10,... | collective-permute-start | bytes 393224 | tf_op jit(solution)/shard_map/ppermute | solution.py:371
  291.1 29.8 %collective-permute-start.12 = (bf16[8,64,128]{2,1,0:T(8,128)(2,1)S(1)}, bf16[8,64,128]{2,1,0:T(8,128)(2,1)S(1)}, u32[]{:S(2)}, u32[]{:S(2)}) collective-permute-start(bf16[8,64,128]{2,1,0:T(8,128)(2,1)S(1)} %get-tuple-element.46), channel_id=1, source_target_pairs={{0,3},{1,2},{2,1},{3,0},{4,7},{5,6},{6,5},{7,4},{8,11},{9,10},{10,... | collective-permute-start | bytes 393224 | tf_op jit(solution)/shard_map/ppermute | solution.py:371
  293.6 20.4 %copy-start.3 = (f32[4,64,128]{2,1,0:T(8,128)S(1)}, f32[4,64,128]{2,1,0:T(8,128)}, u32[]{:S(2)}) copy-start(f32[4,64,128]{2,1,0:T(8,128)} %speed_ref.9) | copy-start | bytes 393220
  293.6 20.4 %copy-start.23 = (bf16[8,64,128]{2,1,0:T(8,128)(2,1)S(1)}, bf16[8,64,128]{2,1,0:T(8,128)(2,1)}, u32[]{:S(2)}) copy-start(bf16[8,64,128]{2,1,0:T(8,128)(2,1)} %copy-done.22) | copy-start | bytes 393220
  (14 other events, 9.9 us)
